TPU v7x, 32 devices: a whole 2x2x4 slice. The times are simulated.
32 devices in a mesh: tm: 4 (over y, core), chan: 8 (over z, x).
Axes of the slice: x: 2, y: 2, z: 4, core: 2. Of those that a mesh axis runs over, the one named last changes fastest.
Arguments:
- recordings: float32 [4, 256, 8, 512], P('tm', None, 'chan')
- gap_start: int32 [4, 256, 8], P('tm', None, 'chan'), may hold values from 0 to 511
- dropout_extent: int32 [4, 256, 8], P('tm', None, 'chan'), may hold values from 0 to 256
- filter_taps: float32 [128], replicated, may hold values from -0.5 to 0.5
- source_channel: int32 [32], P('chan'), may hold values from 0 to 255
- receiver_block: int32 [32], P('chan'), may hold values from 0 to 3
Outputs:
- stacks: float32 [128, 32, 1024], P('tm', 'chan')
All inputs are finite; a program needn't handle non-finite values.
Results may differ from a plain program's by a relative error of at most 0.0031.
Values may be sent and summed in bfloat16 or wider, within the bound.
No kernel may reach another device: no remote copies, remote signals or barrier semaphores. Data moves between devices by JAX's collectives and lax.ppermute only.
A program may use at most 64 MiB of HBM per device.

v0:
```python
import math

import jax
import jax.numpy as jnp
import numpy as np
from jax import lax
from jax.sharding import PartitionSpec as P

BLOCK = 128
MAX_LAG = 512


def passed_along(block, axis, distance):
    devices = range(lax.axis_size(axis))
    route = [(i - distance, i) for i in devices if i - distance in devices]
    return lax.ppermute(block, axis, route)


def valid_mask(starts, lengths, sample_count):
    position = jnp.arange(sample_count, dtype=jnp.int32)
    inside = (position >= starts[..., None]) & (position < starts[..., None] + lengths[..., None])
    return jnp.where(inside, 0.0, 1.0).astype(jnp.float32)


def fir_filter(signal, filter_taps):
    tap_count = filter_taps.shape[0]
    channel_count, sample_count = signal.shape
    pieces = signal.reshape(channel_count, sample_count // tap_count, tap_count)
    earlier = jnp.concatenate([jnp.zeros_like(pieces[:, :1]), pieces[:, :-1]], axis=1)
    position = jnp.arange(tap_count, dtype=jnp.int32)
    offset = position[None, :] - position[:, None]
    present_filter_tap = jnp.where(
        offset >= 0, filter_taps[jnp.clip(offset, 0, tap_count - 1)], 0.0
    )
    carried_tap = jnp.where(
        offset < 0, filter_taps[jnp.clip(offset + tap_count, 0, tap_count - 1)], 0.0
    )
    result = jnp.einsum("cki,im->ckm", pieces, present_filter_tap, precision=lax.Precision.HIGHEST)
    result = result + jnp.einsum(
        "cki,im->ckm", earlier, carried_tap, precision=lax.Precision.HIGHEST
    )
    return result.reshape(channel_count, sample_count)


def normalize_traces(filtered, retained_mask):
    counted = jnp.sum(retained_mask, axis=-1, keepdims=True)
    mean_square = jnp.sum(filtered * filtered * retained_mask, axis=-1, keepdims=True) / counted
    return (filtered * retained_mask * lax.rsqrt(mean_square + 1e-05)).astype(jnp.bfloat16)


def correlate_batch(sources, receivers, max_lag):
    sample_count = sources.shape[-1]
    tile_width = math.gcd(math.gcd(max_lag, sample_count), 128)
    tile_count = sample_count // tile_width + 1
    edge = jnp.zeros((sources.shape[0], tile_width), sources.dtype)
    source_padded = jnp.concatenate([edge, sources, edge], axis=1)
    row_table = (
        np.arange(tile_count * tile_width)[:, None] - np.arange(tile_width)[None, :] + tile_width
    )
    lag_tiles = source_padded[:, row_table]
    lag_pad = jnp.zeros((receivers.shape[0], receivers.shape[1], max_lag), receivers.dtype)
    receivers_padded = jnp.concatenate([lag_pad, receivers, lag_pad], axis=2)
    columns = []
    for lag_block in range(2 * max_lag // tile_width):
        segment_taper = receivers_padded[
            :, :, lag_block * tile_width : lag_block * tile_width + tile_count * tile_width
        ]
        columns.append(
            jnp.einsum("scz,szu->csu", segment_taper, lag_tiles, preferred_element_type=jnp.float32)
        )
    return jnp.concatenate(columns, axis=2)


def select_blocks(blocks, receiver_block, pair_count):
    picked = [
        lax.dynamic_slice_in_dim(blocks, receiver_block[pair_index], 1, axis=0)
        for pair_index in range(pair_count)
    ]
    return jnp.concatenate(picked, axis=0)


def neighbour_blocks(owned_rows):
    return passed_along(owned_rows, "chan", -1)


def local(recordings, gap_start, dropout_extent, filter_taps, source_channel, receiver_block):
    traces = recordings[0, :, 0, :]
    retained_mask = valid_mask(gap_start[0, :, 0], dropout_extent[0, :, 0], traces.shape[1])
    filtered = fir_filter(traces * retained_mask, filter_taps)
    normalized = normalize_traces(filtered, retained_mask)
    round_count, sample_count = normalized.shape
    regrouped = lax.all_to_all(
        normalized.reshape(round_count, 1, sample_count),
        "chan",
        split_axis=0,
        concat_axis=1,
        tiled=True,
    )
    owned_rows = regrouped.reshape(round_count, sample_count)
    sources = owned_rows[source_channel]
    segment_count = lax.axis_size("tm")
    factor = 1.0 / math.sqrt(sample_count * segment_count)
    pair_count = sources.shape[0]
    block_count = round_count // BLOCK
    following = neighbour_blocks(owned_rows)
    blocks = jnp.concatenate([owned_rows, following], axis=0).reshape(
        2 * block_count, BLOCK, sample_count
    )
    receivers = select_blocks(blocks, receiver_block, pair_count)
    stack_terms = correlate_batch(sources, receivers, MAX_LAG) * factor
    stacks = lax.psum_scatter(stack_terms, "tm", scatter_dimension=0, tiled=True)
    return stacks


def solution(mesh):
    return jax.shard_map(
        local,
        mesh=mesh,
        in_specs=(
            P("tm", None, "chan", None),
            P("tm", None, "chan"),
            P("tm", None, "chan"),
            P(),
            P("chan"),
            P("chan"),
        ),
        out_specs=P("tm", "chan", None),
        check_vma=False,
    )
```

profile of v0, /device:TPU:0, one launch (start us, length us, event | category | flops | bytes accessed | tf_op | source)
XLA Modules:
  0.0 605.1 jit_solution(15314912430270999718)
XLA Ops:
  6.6 1.2 copy.46
  7.9 97.2 %gather_fusion = f32[16384]{0:T(1024)S(1)} fusion(f32[128]{0:T(128)S(1)} %copy-done, s32[16384]{0:T(1024)S(1)} %fusion.21), kind=kCustom, calls=%fused_computation | custom fusion | bytes 196608 | tf_op jit(solution)/shard_map/gather | solution.py:33
  105.1 97.2 %gather_fusion.1 = f32[16384]{0:T(1024)S(1)} fusion(f32[128]{0:T(128)S(1)} %copy-done, s32[16384]{0:T(1024)S(1)} %fusion.23), kind=kCustom, calls=%fused_computation.1 | custom fusion | bytes 196608 | tf_op jit(solution)/shard_map/gather | solution.py:36
  202.8 0.6 fusion.25
  203.4 0.7 fusion.16
  204.6 0.5 broadcast.235
  205.1 0.8 reduce.1
  205.9 0.9 reshape.270
  206.8 7.2 %all-to-all-start = ((bf16[8,2,8192]{2,1,0:T(2,128)(2,1)}), bf16[8,2,8192]{2,1,0:T(2,128)(2,1)S(1)}, u32[]{:S(2)}, u32[]{:S(2)}) async-start(bf16[8,2,8192]{2,1,0:T(2,128)(2,1)} %reshape.270), calls=%async_computation | async-start | bytes 524288 | tf_op jit(solution)/shard_map/all_to_all | solution.py:92
  214.2 8.8 %all-to-all-done = bf16[8,2,8192]{2,1,0:T(2,128)(2,1)S(1)} async-done(((bf16[8,2,8192]{2,1,0:T(2,128)(2,1)}), bf16[8,2,8192]{2,1,0:T(2,128)(2,1)S(1)}, u32[]{:S(2)}, u32[]{:S(2)}) %all-to-all-start) | async-done | bytes 262176 | tf_op jit(solution)/shard_map/all_to_all | solution.py:92
  223.4 1.3 collective-permute-start
  224.8 0.7 fusion.47
  233.0 0.6 gather_fusion.2
  233.8 286.2 %gather_fusion.3 = bf16[81920,4]{1,0:T(8,128)(2,1)} fusion(bf16[4,768]{0,1:T(8,128)(2,1)S(1)} %copy.54, s32[81920]{0:T(1024)S(1)} %broadcast_clamp_fusion), kind=kCustom, calls=%fused_computation.3 | custom fusion | bytes 1638400 | tf_op jit(solution)/shard_map/gather | solution.py:60
  520.0 19.5 %copy.55 = bf16[640,128,4]{0,1,2:T(8,128)(2,1)S(1)} copy(bf16[640,128,4]{2,1,0:T(8,128)(2,1)} %bitcast.95) | data formatting | bytes 1310720 | tf_op jit(solution)/shard_map/gather | solution.py:60
  540.6 0.4 fusion.4
  541.0 0.4 fusion.3
  541.4 0.3 fusion.2
  542.1 0.3 fusion
  542.6 2.0 copy.56
  544.7 0.6 copy-done.6
  545.3 0.6 dynamic-slice
  546.5 49.9 %all-reduce.6.cloned.1.call-done = f32[128,4,1024]{2,1,0:T(4,128)} async-done(((f32[128,4,1024]{2,1,0:T(4,128)}), f32[128,4,1024]{2,1,0:T(4,128)}) %all-reduce.6.cloned.1.call-update) | async-done | bytes 2097168
  596.4 1.9 constant_dynamic-slice_fusion.4
  (42 shorter events, 3.3 us)
Async XLA Ops:
  6.5 1.3 copy-start
  105.1 97.2 %copy-start.2 = (s32[1,256,1]{1,2,0:T(1,128)S(1)}, s32[1,256,1]{1,2,0:T(1,128)}, u32[]{:S(2)}) copy-start(s32[1,256,1]{1,2,0:T(1,128)} %param.9) | copy-start | bytes 3076
  105.1 97.2 %copy-start.4 = (s32[1,256,1]{1,2,0:T(1,128)S(1)}, s32[1,256,1]{1,2,0:T(1,128)}, u32[]{:S(2)}) copy-start(s32[1,256,1]{1,2,0:T(1,128)} %param.10) | copy-start | bytes 3076
  203.4 10.7 %copy-start.1 = (s32[81920]{0:T(1024)S(1)}, s32[81920]{0:T(1024)}, u32[]{:S(2)}) copy-start(s32[81920]{0:T(1024)} %constant.48) | copy-start | bytes 983044
  204.2 10.0 %copy-start.5 = (s32[4]{0:T(128)S(1)}, s32[4]{0:T(128)}, u32[]{:S(2)}) copy-start(s32[4]{0:T(128)} %param.12) | copy-start | bytes 52
  205.1 19.6 %copy-start.3 = (s32[4]{0:T(128)S(1)}, s32[4]{0:T(128)}, u32[]{:S(2)}) copy-start(s32[4]{0:T(128)} %param.13) | copy-start | bytes 52
  206.8 16.2 %all-to-all-start = ((bf16[8,2,8192]{2,1,0:T(2,128)(2,1)}), bf16[8,2,8192]{2,1,0:T(2,128)(2,1)S(1)}, u32[]{:S(2)}, u32[]{:S(2)}) async-start(bf16[8,2,8192]{2,1,0:T(2,128)(2,1)} %reshape.270), calls=%async_computation | async-start | bytes 524288 | tf_op jit(solution)/shard_map/all_to_all | solution.py:92
  214.0 382.4 %all-reduce.6.cloned.1.call-start = ((), (), s32[]{:S(2)}) async-start(), calls=%async_computation.1 | async-start | bytes 4194304
  223.4 316.0 %collective-permute-start = (bf16[256,512]{1,0:T(8,128)(2,1)S(1)}, bf16[256,512]{1,0:T(8,128)(2,1)S(1)}, u32[]{:S(2)}, u32[]{:S(2)}) collective-permute-start(bf16[256,512]{1,0:T(8,128)(2,1)S(1)} %bitcast.99), channel_id=1, source_target_pairs={{1,0},{2,1},{3,2},{4,3},{5,4},{6,5},{7,6},{9,8},{10,9},{11,10},{12... | collective-permute-start | bytes 786440 | tf_op jit(solution)/shard_map/ppermute | solution.py:16
  544.6 0.7 copy-start.6
Sparse Core Ops, SparseCore 0:
  544.8 51.5 all-reduce.5
where the time goes:
time: 606 us; the launch traced here: 605 us
  local copies, waits for them, and re-layouts  510 us (84%)
  waiting for transfers between devices  58.7 us (10%)
  between operations  21.9 us (4%)
  starting transfers between devices  8.58 us (1%)
    gather x2, local copies, waits for them, and re-layouts, correlate_batch(): lag_tiles = source_padded[:, row_table]  306 us
    gather x1, local copies, waits for them, and re-layouts, fir_filter(): filter_taps[jnp.clip(offset, 0, tap_count - 1)]  97.2 us
    gather x1, local copies, waits for them, and re-layouts, fir_filter(): filter_taps[jnp.clip(offset + tap_count, 0, tap_count - 1)]  97.2 us
    unnamed x2, waiting for transfers between devices  49.9 us
  transfers between devices with their start and end apart: 3, of which 2 were waited for; matrix products, arithmetic and copies ran while one was open for 51% of the time, Pallas kernels for 0%

commit v1 on v0

v1 whole, which is shorter than its diff:
```python
import math

import jax
import jax.numpy as jnp
from jax import lax
from jax.experimental import pallas as pl
from jax.experimental.pallas import tpu as pltpu
from jax.sharding import PartitionSpec as P

BLOCK = 128
MAX_LAG = 512
LANES = 128
TILE = 256
NEAR = 4


def toeplitz_rows(row, width):
    return pltpu.roll(
        jnp.broadcast_to(row, (LANES, width)), 0, 1, stride=1, stride_axis=0
    )


def normalize_kernel(
    slots, kept, rec_hbm, start_ref, extent_ref, taps_ref, out_ref, rec_ref, sems
):
    blocks = rec_hbm.shape[0]
    rows = blocks * kept
    pieces = rec_hbm.shape[2] // kept
    sample_count = pieces * LANES
    copies = []
    for slot in range(slots):
        copy = pltpu.make_async_copy(rec_hbm.at[:, slot], rec_ref.at[slot], sems.at[slot])
        copy.start()
        copies.append(copy)
    taps = jnp.concatenate([taps_ref[...], jnp.zeros((1, LANES), jnp.float32)], axis=1)
    weights = toeplitz_rows(taps, 2 * LANES)
    starts = start_ref[...].astype(jnp.float32)
    ends = starts + extent_ref[...].astype(jnp.float32)
    round_count = starts.shape[1]
    lane = lax.broadcasted_iota(jnp.int32, (rows, round_count), 1)
    row = lax.broadcasted_iota(jnp.int32, (rows, round_count), 0)
    position = lax.broadcasted_iota(jnp.int32, (rows, LANES), 1).astype(jnp.float32)
    for slot in range(slots):
        own = lane == (row // kept) * (slots * kept) + slot * kept + row % kept
        start = jnp.sum(jnp.where(own, starts, 0.0), axis=1, keepdims=True)
        end = jnp.sum(jnp.where(own, ends, 0.0), axis=1, keepdims=True)
        counted = sample_count - (jnp.minimum(end, float(sample_count)) - start)
        copies[slot].wait()
        flat = rec_ref.at[slot].reshape(rows * pieces, LANES)
        valids = []
        masked = []
        for piece in range(pieces):
            at = position + float(piece * LANES)
            valid = jnp.where((at >= start) & (at < end), 0.0, 1.0)
            valids.append(valid)
            masked.append(flat[pl.ds(piece, rows, stride=pieces), :] * valid)
        spread = jnp.dot(
            jnp.concatenate(masked, axis=0),
            weights,
            preferred_element_type=jnp.float32,
            precision=lax.Precision.HIGHEST,
        )
        kept_parts = []
        squares = jnp.zeros((rows, LANES), jnp.float32)
        for piece in range(pieces):
            filtered = spread[piece * rows : (piece + 1) * rows, :LANES]
            if piece:
                filtered = filtered + spread[(piece - 1) * rows : piece * rows, LANES:]
            filtered = filtered * valids[piece]
            squares = squares + filtered * filtered
            kept_parts.append(filtered)
        mean_square = jnp.sum(squares, axis=1, keepdims=True) / counted
        scale = lax.rsqrt(mean_square + 1e-05)
        normalized = jnp.concatenate(kept_parts, axis=1) * scale
        out_ref[slot] = normalized.astype(out_ref.dtype)


def normalize(recordings, gap_start, dropout_extent, filter_taps, blocks, slots, kept):
    round_count, sample_count = recordings.shape[1], recordings.shape[3]
    pieces = sample_count // LANES
    view = recordings.reshape(blocks, slots, kept * pieces, LANES)

    def body(*refs):
        normalize_kernel(slots, kept, *refs)

    return pl.pallas_call(
        body,
        out_shape=jax.ShapeDtypeStruct((slots, blocks * kept, sample_count), jnp.bfloat16),
        in_specs=[
            pl.BlockSpec(memory_space=pl.ANY),
            pl.BlockSpec(memory_space=pltpu.VMEM),
            pl.BlockSpec(memory_space=pltpu.VMEM),
            pl.BlockSpec(memory_space=pltpu.VMEM),
        ],
        out_specs=pl.BlockSpec(memory_space=pltpu.VMEM),
        scratch_shapes=[
            pltpu.VMEM((slots, blocks, kept * pieces, LANES), jnp.float32),
            pltpu.SemaphoreType.DMA((slots,)),
        ],
        name="normalize",
    )(
        view,
        gap_start.reshape(1, round_count),
        dropout_extent.reshape(1, round_count),
        filter_taps.reshape(1, LANES),
    )


def pick_kernel(units, kept, segments, channel_ref, got_hbm, out_ref, tiles, sems):
    pair_count = channel_ref.shape[0]
    copies = []
    for pair in range(pair_count):
        unit = channel_ref[pair] % units
        for segment in range(segments):
            at = pair * segments + segment
            copy = pltpu.make_async_copy(
                got_hbm.at[segment * units + unit], tiles.at[at], sems.at[at]
            )
            copy.start()
            copies.append(copy)
    for pair in range(pair_count):
        channel = channel_ref[pair]
        wanted = (channel // BLOCK) * kept + ((channel % BLOCK) // units) % kept
        for segment in range(segments):
            at = pair * segments + segment
            copies[at].wait()
            tile = tiles[at].astype(jnp.float32)
            row = lax.broadcasted_iota(jnp.int32, tile.shape, 0)
            found = jnp.sum(jnp.where(row == wanted, tile, 0.0), axis=0, keepdims=True)
            out_ref[at : at + 1, :] = found


def pick_sources(source_channel, got, units, kept, segments):
    pair_count = source_channel.shape[0]
    chunk_rows, sample_count = got.shape[1:]
    count = pair_count * segments

    def body(*refs):
        pick_kernel(units, kept, segments, *refs)

    return pl.pallas_call(
        body,
        out_shape=jax.ShapeDtypeStruct((count, sample_count), jnp.float32),
        in_specs=[
            pl.BlockSpec(memory_space=pltpu.SMEM),
            pl.BlockSpec(memory_space=pl.ANY),
        ],
        out_specs=pl.BlockSpec(memory_space=pltpu.VMEM),
        scratch_shapes=[
            pltpu.VMEM((count, chunk_rows, sample_count), jnp.bfloat16),
            pltpu.SemaphoreType.DMA((count,)),
        ],
        name="pick_sources",
    )(source_channel, got)


def merge_in_kernel(got_ref, merged_ref, units):
    segments = merged_ref.shape[1]
    upper = lax.broadcasted_iota(jnp.int32, (8, got_ref.shape[2]), 0) < 4
    for segment in range(segments):
        for first in range(0, units, 4):
            parts = [[] for _ in range(NEAR)]
            for unit in (first, first + 2):
                low = got_ref[segment * units + unit].astype(jnp.float32)
                high = got_ref[segment * units + unit + 1].astype(jnp.float32)
                for half in range(2):
                    a = low[8 * half : 8 * half + 8]
                    b = high[8 * half : 8 * half + 8]
                    parts[2 * half].append(jnp.where(upper, a, pltpu.roll(b, 4, 0)))
                    parts[2 * half + 1].append(jnp.where(upper, pltpu.roll(a, 4, 0), b))
            for block in range(NEAR):
                merged_ref[block, segment, first * 4 : first * 4 + 16, :] = jnp.concatenate(
                    parts[block], axis=0
                ).astype(jnp.bfloat16)


def correlate_kernel(
    owned, kept, units, merged_here, channel_ref, block_ref, got_ref, source_ref, out_ref, *scratch
):
    if merged_here:
        merged_ref, lines_ref = scratch
        merge_in_kernel(got_ref, merged_ref, units)
    else:
        merged_ref, (lines_ref,) = got_ref, scratch
    segments, _, sample_count = merged_ref.shape[1:]
    pair_count = channel_ref.shape[0]
    factor = 1.0 / math.sqrt(sample_count * segments)
    halves = sample_count // TILE
    lag_tiles = 2 * MAX_LAG // TILE
    spare = jnp.zeros((1, LANES), jnp.float32)
    edge = jnp.zeros((LANES, LANES), jnp.bfloat16)
    for pair in range(pair_count):
        holder = (channel_ref[pair] % BLOCK) // owned
        block = block_ref[pair]
        sums = [None] * lag_tiles
        for segment in range(segments):
            at = pair * segments + segment
            line = source_ref[holder, at : at + 1, :].astype(jnp.float32)
            moved = toeplitz_rows(
                jnp.concatenate([line, spare], axis=1), sample_count + LANES
            ).astype(jnp.bfloat16)
            padded = jnp.concatenate([edge, moved, edge], axis=1)
            rows = merged_ref[block, segment]
            taken = jnp.concatenate(
                [rows[:, half * TILE : (half + 1) * TILE] for half in range(halves)], axis=0
            )
            for step in range(halves + 1):
                low = step * TILE
                tile = jnp.concatenate(
                    [padded[:, low + LANES : low + LANES + TILE], padded[:, low : low + TILE]],
                    axis=0,
                )
                product = lax.dot_general(
                    taken, tile, (((1,), (1,)), ((), ())), preferred_element_type=jnp.float32
                )
                for half in range(halves):
                    lag_tile = half + MAX_LAG // TILE - step
                    part = product[half * owned : (half + 1) * owned]
                    old = sums[lag_tile]
                    sums[lag_tile] = part if old is None else old + part
        across = owned // kept
        for lag_tile in range(lag_tiles):
            for part in range(TILE // LANES):
                low = part * LANES
                lines_ref[...] = sums[lag_tile][:, low : low + LANES] * factor
                low = low + lag_tile * TILE
                for place in range(kept):
                    out_ref[place * across : (place + 1) * across, pair, low : low + LANES] = (
                        lines_ref[pl.ds(place, across, stride=kept), :]
                    )


def correlate(source_channel, receiver_block, got, sources, owned, kept, units, merged_here):
    pair_count = source_channel.shape[0]
    segments, sample_count = sources.shape[1] // pair_count, sources.shape[2]

    def body(*refs):
        correlate_kernel(owned, kept, units, merged_here, *refs)

    scratch = [pltpu.VMEM((owned, LANES), jnp.float32)]
    if merged_here:
        scratch.insert(0, pltpu.VMEM((NEAR, segments, owned, sample_count), jnp.bfloat16))
    return pl.pallas_call(
        body,
        out_shape=jax.ShapeDtypeStruct((owned, pair_count, 2 * MAX_LAG), jnp.float32),
        in_specs=[
            pl.BlockSpec(memory_space=pltpu.SMEM),
            pl.BlockSpec(memory_space=pltpu.SMEM),
            pl.BlockSpec(memory_space=pltpu.VMEM),
            pl.BlockSpec(memory_space=pltpu.VMEM),
        ],
        out_specs=pl.BlockSpec(memory_space=pltpu.VMEM),
        scratch_shapes=scratch,
        name="correlate",
    )(source_channel, receiver_block, got, sources)


def local(recordings, gap_start, dropout_extent, filter_taps, source_channel, receiver_block):
    round_count, sample_count = recordings.shape[1], recordings.shape[3]
    segments = lax.axis_size("tm")
    units = lax.axis_size("chan")
    groups = units
    blocks = round_count * units // BLOCK
    near = blocks // groups
    owned = BLOCK // segments
    rounds_block = BLOCK // units
    slots = min(segments, rounds_block)
    kept = rounds_block // slots
    normalized = normalize(
        recordings, gap_start, dropout_extent, filter_taps, blocks, slots, kept
    )
    beyond = jnp.zeros((slots, near * kept, sample_count), normalized.dtype)
    extended = jnp.concatenate([normalized, beyond], axis=1)
    windows = jnp.stack(
        [
            extended[:, group * near * kept : (group + 2) * near * kept]
            for group in range(groups)
        ],
        axis=1,
    )
    sent = jnp.repeat(windows, segments // slots, axis=0)
    got = lax.all_to_all(
        sent.reshape(segments * groups, NEAR * kept, sample_count),
        ("tm", "chan"),
        split_axis=0,
        concat_axis=0,
        tiled=True,
    )
    picked = pick_sources(source_channel, got, units, kept, segments)
    sources = lax.all_gather(picked.astype(jnp.bfloat16), "tm")
    merged_here = kept == 4 and owned == 4 * units
    if not merged_here:
        across = owned // kept
        apart = got.reshape(segments, units, NEAR, kept, sample_count)
        first = lax.axis_index("tm") * owned % units
        apart = lax.dynamic_slice_in_dim(apart, first, across, axis=1)
        got = apart.transpose(2, 0, 1, 3, 4).reshape(NEAR, segments, owned, sample_count)
    return correlate(
        source_channel, receiver_block, got, sources, owned, kept, units, merged_here
    )


def solution(mesh):
    return jax.shard_map(
        local,
        mesh=mesh,
        in_specs=(
            P("tm", None, "chan", None),
            P("tm", None, "chan"),
            P("tm", None, "chan"),
            P(),
            P("chan"),
            P("chan"),
        ),
        out_specs=P("tm", "chan", None),
        check_vma=False,
    )
```

time: 606 us -> 44.7 us (0.07)
  local copies, waits for them, and re-layouts: 510 us -> 2.67 us
  waiting for transfers between devices: 58.7 us -> 0 us
  blocking collectives: 0 us -> 29.2 us
  between operations: 21.9 us -> 0.07 us
  Pallas kernels: 0 us -> 11.5 us
  starting transfers between devices: 8.58 us -> 0 us
    gather x5 -> x0, local copies, waits for them, and re-layouts: 501 us -> none  [the longest x2 306 us: correlate_batch(): lag_tiles = source_padded[:, row_table]]
    unnamed x2 -> x0, waiting for transfers between devices: 49.9 us -> none
    all_to_all x0 -> x1, blocking collectives: none -> 23.6 us  [local(): lax.all_to_all(sent.reshape(segments * groups, NEAR * kept, sample_count)...]
    pallas_call x0 -> x3, Pallas kernels: none -> 11.5 us  [the longest x1 4.85 us: normalize(): pl.pallas_call(body, out_shape=jax.ShapeDtypeStruct((slots, blocks * kept...]
    all_to_all x1 -> x0, waiting for transfers between devices: 8.79 us -> none  [local(): lax.all_to_all(normalized.reshape(round_count, 1, sample_count), 'chan',...]
    all_to_all x1 -> x0, starting transfers between devices: 7.25 us -> none  [local(): lax.all_to_all(normalized.reshape(round_count, 1, sample_count), 'chan',...]
  transfers between devices with their start and end apart: 3 -> 0, of which waited for: 2 -> 0; matrix products, arithmetic and copies ran while one was open for 51% -> 0% of each run, Pallas kernels for 0% -> 0%
where the time goes in v1:
time: 44.7 us; the launch traced here: 44.3 us
  blocking collectives  29.2 us (65%)
  Pallas kernels  11.5 us (26%)
  local copies, waits for them, and re-layouts  2.67 us (6%)
  other arithmetic  0.76 us (2%)
    all_to_all x1, blocking collectives, local(): lax.all_to_all(sent.reshape(segments * groups, NEAR * kept, sample_count)...  23.6 us
    all_gather x1, blocking collectives, local(): sources = lax.all_gather(picked.astype(jnp.bfloat16), 'tm')  5.68 us
    pallas_call x1, Pallas kernels, normalize(): pl.pallas_call(body, out_shape=jax.ShapeDtypeStruct((slots, blocks * kept...  4.85 us
    pallas_call x1, Pallas kernels, correlate(): pl.pallas_call(body, out_shape=jax.ShapeDtypeStruct((owned, pair_count, 2...  4.26 us
    unnamed x9, local copies, waits for them, and re-layouts  2.63 us
    pallas_call x1, Pallas kernels, pick_sources(): pl.pallas_call(body, out_shape=jax.ShapeDtypeStruct((count, sample_count)...  2.4 us

profile of v1, /device:TPU:0, one launch (start us, length us, event | category | flops | bytes accessed | tf_op | source)
XLA Modules:
  0.0 44.3 jit_solution(10164009298438954161)
XLA Ops:
  0.0 4.8 %normalize.1 = bf16[4,64,512]{2,1,0:T(8,128)(2,1)} custom-call(f32[16,4,16,128]{3,2,1,0:T(8,128)} %bitcast.39, s32[1,256]{1,0:T(1,128)} %bitcast.41, s32[1,256]{1,0:T(1,128)} %bitcast.42, f32[1,128]{1,0:T(1,128)} %bitcast.43), custom_call_target="tpu_custom_call" | custom-call | tf_op jit(solution)/shard_map/normalize/pallas_call | solution.py:86
  4.9 0.0 copy-start
  4.9 0.9 %fusion.8 = bf16[4,8,16,512]{3,2,0,1:T(8,128)(2,1)S(1)} fusion(bf16[4,64,512]{2,1,0:T(8,128)(2,1)} %normalize.1), kind=kLoop, calls=%fused_computation.16 | loop fusion | bytes 131072
  5.8 0.8 %fusion.7 = bf16[4,8,16,512]{3,2,0,1:T(8,128)(2,1)S(1)} fusion(bf16[4,8,16,512]{3,2,0,1:T(8,128)(2,1)S(1)} %fusion.8, bf16[4,64,512]{2,1,0:T(8,128)(2,1)} %normalize.1), kind=kLoop, calls=%fused_computation.14 | loop fusion | bytes 131072
  6.6 0.8 %fusion.6 = bf16[4,8,16,512]{3,2,0,1:T(8,128)(2,1)S(1)} fusion(bf16[4,8,16,512]{3,2,0,1:T(8,128)(2,1)S(1)} %fusion.7, bf16[4,64,512]{2,1,0:T(8,128)(2,1)} %normalize.1), kind=kLoop, calls=%fused_computation.12 | loop fusion | bytes 131072
  7.5 0.0 copy-done
  7.6 23.6 %all_to_all.5.refs_1_.refs_2_ = bf16[32,16,512]{2,1,0:T(8,128)(2,1)} all-to-all(bf16[32,16,512]{2,1,0:T(8,128)(2,1)S(1)} %bitcast.38), channel_id=1, replica_groups=mesh['tm'=4,'chan'=8] {'tm','chan'}, dimensions={0} | all-to-all | bytes 1048576 | tf_op jit(solution)/shard_map/all_to_all | solution.py:282
  31.1 2.4 %pick_sources.1 = f32[16,512]{1,0:T(8,128)} custom-call(s32[4]{0:T(128)} %refs_0_.3, bf16[32,16,512]{2,1,0:T(8,128)(2,1)} %all_to_all.5.refs_1_.refs_2_), custom_call_target="tpu_custom_call" | custom-call | tf_op jit(solution)/shard_map/pick_sources/pallas_call | solution.py:141
  33.6 0.8 %convert_element_type.3 = bf16[16,512]{1,0:T(8,128)(2,1)S(1)} convert(f32[16,512]{1,0:T(8,128)} %pick_sources.1) | non-fusion elementwise | flops 8192 | bytes 49152 | tf_op jit(solution)/shard_map/convert_element_type | solution.py:290
  34.3 5.7 %all-gather = bf16[64,512]{1,0:T(8,128)(2,1)} all-gather(bf16[16,512]{1,0:T(8,128)(2,1)S(1)} %convert_element_type.3), channel_id=2, replica_groups=mesh['tm'=4,'chan'=8] {'tm'}, dimensions={0}, use_global_device_ids=true | all-gather | bytes 81920 | tf_op jit(solution)/shard_map/all_gather | solution.py:290
  40.0 4.3 %correlate.1 = f32[32,4,1024]{2,1,0:T(4,128)} custom-call(s32[4]{0:T(128)} %refs_0_.3, s32[4]{0:T(128)} %refs_1_.1, bf16[32,16,512]{2,1,0:T(8,128)(2,1)} %all_to_all.5.refs_1_.refs_2_, bf16[4,16,512]{2,1,0:T(8,128)(2,1)} %bitcast.40), custom_call_target="tpu_custom_call" | custom-call | tf_op jit(solution)/shard_map/correlate/pallas_call | solution.py:243
  (6 shorter events, 0.1 us)
Async XLA Ops:
  4.9 2.6 %copy-start = (bf16[4,64,512]{2,1,0:T(8,128)(2,1)S(1)}, bf16[4,64,512]{2,1,0:T(8,128)(2,1)}, u32[]{:S(2)}) copy-start(bf16[4,64,512]{2,1,0:T(8,128)(2,1)} %normalize.1) | copy-start | bytes 786436

commit v2 on v1

--- a/solution.py
+++ b/solution.py
@@ -127,7 +127,7 @@
             tile = tiles[at].astype(jnp.float32)
             row = lax.broadcasted_iota(jnp.int32, tile.shape, 0)
             found = jnp.sum(jnp.where(row == wanted, tile, 0.0), axis=0, keepdims=True)
-            out_ref[at : at + 1, :] = found
+            out_ref[at : at + 1, :] = found.astype(out_ref.dtype)
 
 
 def pick_sources(source_channel, got, units, kept, segments):
@@ -140,7 +140,7 @@
 
     return pl.pallas_call(
         body,
-        out_shape=jax.ShapeDtypeStruct((count, sample_count), jnp.float32),
+        out_shape=jax.ShapeDtypeStruct((count, sample_count), jnp.bfloat16),
         in_specs=[
             pl.BlockSpec(memory_space=pltpu.SMEM),
             pl.BlockSpec(memory_space=pl.ANY),
@@ -154,34 +154,30 @@
     )(source_channel, got)
 
 
-def merge_in_kernel(got_ref, merged_ref, units):
+def merge_in_kernel(got_refs, merged_ref, units):
     segments = merged_ref.shape[1]
-    upper = lax.broadcasted_iota(jnp.int32, (8, got_ref.shape[2]), 0) < 4
-    for segment in range(segments):
-        for first in range(0, units, 4):
-            parts = [[] for _ in range(NEAR)]
-            for unit in (first, first + 2):
-                low = got_ref[segment * units + unit].astype(jnp.float32)
-                high = got_ref[segment * units + unit + 1].astype(jnp.float32)
-                for half in range(2):
-                    a = low[8 * half : 8 * half + 8]
-                    b = high[8 * half : 8 * half + 8]
-                    parts[2 * half].append(jnp.where(upper, a, pltpu.roll(b, 4, 0)))
-                    parts[2 * half + 1].append(jnp.where(upper, pltpu.roll(a, 4, 0), b))
-            for block in range(NEAR):
-                merged_ref[block, segment, first * 4 : first * 4 + 16, :] = jnp.concatenate(
-                    parts[block], axis=0
-                ).astype(jnp.bfloat16)
-
-
-def correlate_kernel(
-    owned, kept, units, merged_here, channel_ref, block_ref, got_ref, source_ref, out_ref, *scratch
-):
+    upper = lax.broadcasted_iota(jnp.int32, (8, merged_ref.shape[3]), 0) < 4
+    for group, got_ref in enumerate(got_refs):
+        for segment in range(segments):
+            for first in range(0, units, 4):
+                parts = [[], []]
+                for unit in (first, first + 2):
+                    a = got_ref[segment * units + unit].astype(jnp.float32)
+                    b = got_ref[segment * units + unit + 1].astype(jnp.float32)
+                    parts[0].append(jnp.where(upper, a, pltpu.roll(b, 4, 0)))
+                    parts[1].append(jnp.where(upper, pltpu.roll(a, 4, 0), b))
+                for block in range(2):
+                    merged_ref[2 * group + block, segment, first * 4 : first * 4 + 16, :] = (
+                        jnp.concatenate(parts[block], axis=0).astype(jnp.bfloat16)
+                    )
+
+
+def correlate_kernel(owned, kept, units, merged_here, channel_ref, block_ref, source_ref, *refs):
     if merged_here:
-        merged_ref, lines_ref = scratch
-        merge_in_kernel(got_ref, merged_ref, units)
+        own_ref, next_ref, out_ref, lines_ref, merged_ref = refs
+        merge_in_kernel((own_ref, next_ref), merged_ref, units)
     else:
-        merged_ref, (lines_ref,) = got_ref, scratch
+        merged_ref, out_ref, lines_ref = refs
     segments, _, sample_count = merged_ref.shape[1:]
     pair_count = channel_ref.shape[0]
     factor = 1.0 / math.sqrt(sample_count * segments)
@@ -230,29 +226,26 @@
                     )
 
 
-def correlate(source_channel, receiver_block, got, sources, owned, kept, units, merged_here):
+def correlate(source_channel, receiver_block, sources, receivers, owned, kept, units):
     pair_count = source_channel.shape[0]
     segments, sample_count = sources.shape[1] // pair_count, sources.shape[2]
+    merged_here = len(receivers) == 2
 
     def body(*refs):
         correlate_kernel(owned, kept, units, merged_here, *refs)
 
     scratch = [pltpu.VMEM((owned, LANES), jnp.float32)]
     if merged_here:
-        scratch.insert(0, pltpu.VMEM((NEAR, segments, owned, sample_count), jnp.bfloat16))
+        scratch.append(pltpu.VMEM((NEAR, segments, owned, sample_count), jnp.bfloat16))
     return pl.pallas_call(
         body,
         out_shape=jax.ShapeDtypeStruct((owned, pair_count, 2 * MAX_LAG), jnp.float32),
-        in_specs=[
-            pl.BlockSpec(memory_space=pltpu.SMEM),
-            pl.BlockSpec(memory_space=pltpu.SMEM),
-            pl.BlockSpec(memory_space=pltpu.VMEM),
-            pl.BlockSpec(memory_space=pltpu.VMEM),
-        ],
+        in_specs=[pl.BlockSpec(memory_space=pltpu.SMEM)] * 2
+        + [pl.BlockSpec(memory_space=pltpu.VMEM)] * (1 + len(receivers)),
         out_specs=pl.BlockSpec(memory_space=pltpu.VMEM),
         scratch_shapes=scratch,
         name="correlate",
-    )(source_channel, receiver_block, got, sources)
+    )(source_channel, receiver_block, sources, *receivers)
 
 
 def local(recordings, gap_start, dropout_extent, filter_taps, source_channel, receiver_block):
@@ -269,35 +262,28 @@
     normalized = normalize(
         recordings, gap_start, dropout_extent, filter_taps, blocks, slots, kept
     )
-    beyond = jnp.zeros((slots, near * kept, sample_count), normalized.dtype)
-    extended = jnp.concatenate([normalized, beyond], axis=1)
-    windows = jnp.stack(
-        [
-            extended[:, group * near * kept : (group + 2) * near * kept]
-            for group in range(groups)
-        ],
-        axis=1,
-    )
-    sent = jnp.repeat(windows, segments // slots, axis=0)
+    sent = normalized.reshape(slots, groups, near * kept, sample_count)
+    sent = jnp.repeat(sent, segments // slots, axis=0) if segments > slots else sent
     got = lax.all_to_all(
-        sent.reshape(segments * groups, NEAR * kept, sample_count),
+        sent.reshape(segments * groups, near * kept, sample_count),
         ("tm", "chan"),
         split_axis=0,
         concat_axis=0,
         tiled=True,
     )
+    following = lax.ppermute(got, "chan", [(group, group - 1) for group in range(1, groups)])
     picked = pick_sources(source_channel, got, units, kept, segments)
-    sources = lax.all_gather(picked.astype(jnp.bfloat16), "tm")
-    merged_here = kept == 4 and owned == 4 * units
-    if not merged_here:
+    sources = lax.all_gather(picked, "tm")
+    receivers = (got, following)
+    if kept != 4 or owned != 4 * units or near != 2:
         across = owned // kept
-        apart = got.reshape(segments, units, NEAR, kept, sample_count)
         first = lax.axis_index("tm") * owned % units
-        apart = lax.dynamic_slice_in_dim(apart, first, across, axis=1)
-        got = apart.transpose(2, 0, 1, 3, 4).reshape(NEAR, segments, owned, sample_count)
-    return correlate(
-        source_channel, receiver_block, got, sources, owned, kept, units, merged_here
-    )
+        apart = [x.reshape(segments, units, near, kept, sample_count) for x in receivers]
+        apart = lax.dynamic_slice_in_dim(jnp.concatenate(apart, axis=2), first, across, axis=1)
+        receivers = (
+            apart.transpose(2, 0, 1, 3, 4).reshape(2 * near, segments, owned, sample_count),
+        )
+    return correlate(source_channel, receiver_block, sources, receivers, owned, kept, units)
 
 
 def solution(mesh):

time: 44.7 us -> 38.4 us (0.86)
  blocking collectives: 29.2 us -> 23.9 us
  local copies, waits for them, and re-layouts: 2.67 us -> 0.71 us
  starting transfers between devices: 0 us -> 1.28 us
  other arithmetic: 0.76 us -> 0 us
    all_to_all x1, blocking collectives: 23.6 us -> 18 us  [local(): lax.all_to_all(sent.reshape(segments * groups, near * kept, sample_count)...]
    unnamed x9 -> x4, local copies, waits for them, and re-layouts: 2.63 us -> 0.71 us
    ppermute x0 -> x1, starting transfers between devices: none -> 1.28 us  [local(): lax.ppermute(got, 'chan', [(group, group - 1) for group in range(1, group...]
    convert_element_type x1 -> x0, other arithmetic: 0.76 us -> none  [local(): sources = lax.all_gather(picked.astype(jnp.bfloat16), 'tm')]
  transfers between devices with their start and end apart: 0 -> 1, of which waited for: 0 -> 1; matrix products, arithmetic and copies ran while one was open for 0% -> 0% of each run, Pallas kernels for 0% -> 6%
where the time goes in v2:
time: 38.4 us; the launch traced here: 37.7 us
  blocking collectives  23.9 us (62%)
  Pallas kernels  11.5 us (30%)
  starting transfers between devices  1.28 us (3%)
  local copies, waits for them, and re-layouts  0.71 us (2%)
    all_to_all x1, blocking collectives, local(): lax.all_to_all(sent.reshape(segments * groups, near * kept, sample_count)...  18 us
    all_gather x1, blocking collectives, local(): sources = lax.all_gather(picked, 'tm')  5.9 us
    pallas_call x1, Pallas kernels, normalize(): pl.pallas_call(body, out_shape=jax.ShapeDtypeStruct((slots, blocks * kept...  4.85 us
    pallas_call x1, Pallas kernels, correlate(): pl.pallas_call(body, out_shape=jax.ShapeDtypeStruct((owned, pair_count, 2...  4.28 us
    pallas_call x1, Pallas kernels, pick_sources(): pl.pallas_call(body, out_shape=jax.ShapeDtypeStruct((count, sample_count)...  2.34 us
    ppermute x1, starting transfers between devices, local(): lax.ppermute(got, 'chan', [(group, group - 1) for group in range(1, group...  1.28 us
  transfers between devices with their start and end apart: 1, of which 1 were waited for; matrix products, arithmetic and copies ran while one was open for 0% of the time, Pallas kernels for 6%

profile of v2, /device:TPU:0, one launch (start us, length us, event | category | flops | bytes accessed | tf_op | source)
XLA Modules:
  0.0 37.7 jit_solution(1399746719993971811)
XLA Ops:
  0.0 4.8 %normalize.1 = bf16[4,64,512]{2,1,0:T(8,128)(2,1)} custom-call(f32[16,4,16,128]{3,2,1,0:T(8,128)} %bitcast.7, s32[1,256]{1,0:T(1,128)} %bitcast.9, s32[1,256]{1,0:T(1,128)} %bitcast.10, f32[1,128]{1,0:T(1,128)} %bitcast.11), custom_call_target="tpu_custom_call" | custom-call | tf_op jit(solution)/shard_map/normalize/pallas_call | solution.py:86
  4.9 18.0 %all_to_all.5.refs_1_.refs_3_ = bf16[32,8,512]{2,1,0:T(8,128)(2,1)S(1)} all-to-all(bf16[32,8,512]{2,1,0:T(8,128)(2,1)} %bitcast.6), channel_id=1, replica_groups=mesh['tm'=4,'chan'=8] {'tm','chan'}, dimensions={0} | all-to-all | bytes 524288 | tf_op jit(solution)/shard_map/all_to_all | solution.py:267
  22.8 0.0 copy-start
  22.8 1.3 %collective-permute-start = (bf16[32,8,512]{2,1,0:T(8,128)(2,1)S(1)}, bf16[32,8,512]{2,1,0:T(8,128)(2,1)S(1)}, u32[]{:S(2)}, u32[]{:S(2)}) collective-permute-start(bf16[32,8,512]{2,1,0:T(8,128)(2,1)S(1)} %all_to_all.5.refs_1_.refs_3_), channel_id=1, source_target_pairs={{1,0},{2,1},{3,2},{4,3},{5,4},{6,5},{7,6},{9,8},{10,9},{11,10},{12... | collective-permute-start | bytes 786440 | tf_op jit(solution)/shard_map/ppermute | solution.py:274
  24.1 0.0 copy-done
  24.1 2.3 %pick_sources.1 = bf16[16,512]{1,0:T(8,128)(2,1)} custom-call(s32[4]{0:T(128)} %refs_0_.3, bf16[32,8,512]{2,1,0:T(8,128)(2,1)} %copy-done), custom_call_target="tpu_custom_call" | custom-call | tf_op jit(solution)/shard_map/pick_sources/pallas_call | solution.py:141
  26.5 5.9 %all-gather = bf16[64,512]{1,0:T(8,128)(2,1)} all-gather(bf16[16,512]{1,0:T(8,128)(2,1)} %pick_sources.1), channel_id=2, replica_groups=mesh['tm'=4,'chan'=8] {'tm'}, dimensions={0}, use_global_device_ids=true | all-gather | bytes 81920 | tf_op jit(solution)/shard_map/all_gather | solution.py:276
  32.4 0.3 collective-permute-done.refs_4_
  32.7 0.0 copy-start.1
  32.7 0.7 %copy-done.1 = bf16[32,8,512]{2,1,0:T(8,128)(2,1)} copy-done((bf16[32,8,512]{2,1,0:T(8,128)(2,1)}, bf16[32,8,512]{2,1,0:T(8,128)(2,1)S(1)}, u32[]{:S(2)}) %copy-start.1) | copy-done | bytes 262168
  33.4 4.3 %correlate.1 = f32[32,4,1024]{2,1,0:T(4,128)} custom-call(s32[4]{0:T(128)} %refs_0_.3, s32[4]{0:T(128)} %refs_1_.1, bf16[4,16,512]{2,1,0:T(8,128)(2,1)} %bitcast.8, bf16[32,8,512]{2,1,0:T(8,128)(2,1)} %copy-done, bf16[32,8,512]{2,1,0:T(8,128)(2,1)} %copy-done.1), custom_call_target="tpu_custom_call" | custom-call | tf_op jit(solution)/shard_map/correlate/pallas_call | solution.py:240
Async XLA Ops:
  22.8 1.3 %copy-start = (bf16[32,8,512]{2,1,0:T(8,128)(2,1)}, bf16[32,8,512]{2,1,0:T(8,128)(2,1)S(1)}, u32[]{:S(2)}) copy-start(bf16[32,8,512]{2,1,0:T(8,128)(2,1)S(1)} %all_to_all.5.refs_1_.refs_3_) | copy-start | bytes 786436
  22.8 9.8 %collective-permute-start = (bf16[32,8,512]{2,1,0:T(8,128)(2,1)S(1)}, bf16[32,8,512]{2,1,0:T(8,128)(2,1)S(1)}, u32[]{:S(2)}, u32[]{:S(2)}) collective-permute-start(bf16[32,8,512]{2,1,0:T(8,128)(2,1)S(1)} %all_to_all.5.refs_1_.refs_3_), channel_id=1, source_target_pairs={{1,0},{2,1},{3,2},{4,3},{5,4},{6,5},{7,6},{9,8},{10,9},{11,10},{12... | collective-permute-start | bytes 786440 | tf_op jit(solution)/shard_map/ppermute | solution.py:274
  32.7 0.7 %copy-start.1 = (bf16[32,8,512]{2,1,0:T(8,128)(2,1)}, bf16[32,8,512]{2,1,0:T(8,128)(2,1)S(1)}, u32[]{:S(2)}) copy-start(bf16[32,8,512]{2,1,0:T(8,128)(2,1)S(1)} %collective-permute-done.refs_4_) | copy-start | bytes 786436

commit v3 on v2

--- a/solution.py
+++ b/solution.py
@@ -14,9 +14,13 @@
 NEAR = 4
 
 
-def toeplitz_rows(row, width):
+def near_core(x):
+    return pltpu.with_memory_space_constraint(x, pltpu.VMEM)
+
+
+def toeplitz_rows(row, width, first=0):
     return pltpu.roll(
-        jnp.broadcast_to(row, (LANES, width)), 0, 1, stride=1, stride_axis=0
+        jnp.broadcast_to(row, (LANES, width)), first, 1, stride=1, stride_axis=0
     )
 
 
@@ -40,12 +44,16 @@
     lane = lax.broadcasted_iota(jnp.int32, (rows, round_count), 1)
     row = lax.broadcasted_iota(jnp.int32, (rows, round_count), 0)
     position = lax.broadcasted_iota(jnp.int32, (rows, LANES), 1).astype(jnp.float32)
+    spans = []
     for slot in range(slots):
         own = lane == (row // kept) * (slots * kept) + slot * kept + row % kept
         start = jnp.sum(jnp.where(own, starts, 0.0), axis=1, keepdims=True)
         end = jnp.sum(jnp.where(own, ends, 0.0), axis=1, keepdims=True)
-        counted = sample_count - (jnp.minimum(end, float(sample_count)) - start)
-        copies[slot].wait()
+        spans.append((start, end, sample_count - (jnp.minimum(end, float(sample_count)) - start)))
+    for copy in copies:
+        copy.wait()
+    for slot in range(slots):
+        start, end, counted = spans[slot]
         flat = rec_ref.at[slot].reshape(rows * pieces, LANES)
         valids = []
         masked = []
@@ -85,7 +93,7 @@
 
     return pl.pallas_call(
         body,
-        out_shape=jax.ShapeDtypeStruct((slots, blocks * kept, sample_count), jnp.bfloat16),
+        out_shape=pltpu.VMEM((slots, blocks * kept, sample_count), jnp.bfloat16),
         in_specs=[
             pl.BlockSpec(memory_space=pl.ANY),
             pl.BlockSpec(memory_space=pltpu.VMEM),
@@ -106,52 +114,46 @@
     )
 
 
-def pick_kernel(units, kept, segments, channel_ref, got_hbm, out_ref, tiles, sems):
-    pair_count = channel_ref.shape[0]
-    copies = []
-    for pair in range(pair_count):
-        unit = channel_ref[pair] % units
+def pick_kernel(units, kept, segments, channel_ref, got_ref, out_ref):
+    sample_count = got_ref.shape[2]
+    shape = got_ref.shape[1:]
+    row = lax.broadcasted_iota(jnp.int32, shape, 0)
+    found = []
+    for pair in range(channel_ref.shape[0]):
+        channel = channel_ref[pair]
+        unit = channel % units
+        wanted = row == (channel // BLOCK) * kept + ((channel % BLOCK) // units) % kept
         for segment in range(segments):
-            at = pair * segments + segment
-            copy = pltpu.make_async_copy(
-                got_hbm.at[segment * units + unit], tiles.at[at], sems.at[at]
-            )
-            copy.start()
-            copies.append(copy)
-    for pair in range(pair_count):
-        channel = channel_ref[pair]
-        wanted = (channel // BLOCK) * kept + ((channel % BLOCK) // units) % kept
-        for segment in range(segments):
-            at = pair * segments + segment
-            copies[at].wait()
-            tile = tiles[at].astype(jnp.float32)
-            row = lax.broadcasted_iota(jnp.int32, tile.shape, 0)
-            found = jnp.sum(jnp.where(row == wanted, tile, 0.0), axis=0, keepdims=True)
-            out_ref[at : at + 1, :] = found.astype(out_ref.dtype)
+            tile = got_ref[segment * units + unit].astype(jnp.float32)
+            found.append(jnp.sum(jnp.where(wanted, tile, 0.0), axis=0, keepdims=True))
+    lines = jnp.concatenate(found, axis=0).astype(jnp.bfloat16)
+    swap = lax.broadcasted_iota(jnp.int32, (LANES, LANES), 0) + lax.broadcasted_iota(
+        jnp.int32, (LANES, LANES), 1
+    )
+    swap = jnp.where(swap == LANES - 1, 1.0, 0.0).astype(jnp.bfloat16)
+    for low in range(0, sample_count, LANES):
+        high = sample_count - low
+        out_ref[:, low : low + LANES] = jnp.dot(
+            lines[:, high - LANES : high], swap, preferred_element_type=jnp.float32
+        ).astype(out_ref.dtype)
 
 
 def pick_sources(source_channel, got, units, kept, segments):
-    pair_count = source_channel.shape[0]
-    chunk_rows, sample_count = got.shape[1:]
-    count = pair_count * segments
+    count = source_channel.shape[0] * segments
 
     def body(*refs):
         pick_kernel(units, kept, segments, *refs)
 
     return pl.pallas_call(
         body,
-        out_shape=jax.ShapeDtypeStruct((count, sample_count), jnp.bfloat16),
+        out_shape=pltpu.VMEM((count, got.shape[2]), jnp.bfloat16),
         in_specs=[
             pl.BlockSpec(memory_space=pltpu.SMEM),
-            pl.BlockSpec(memory_space=pl.ANY),
+            pl.BlockSpec(memory_space=pltpu.VMEM),
         ],
         out_specs=pl.BlockSpec(memory_space=pltpu.VMEM),
-        scratch_shapes=[
-            pltpu.VMEM((count, chunk_rows, sample_count), jnp.bfloat16),
-            pltpu.SemaphoreType.DMA((count,)),
-        ],
         name="pick_sources",
-    )(source_channel, got)
+    )(source_channel, near_core(got))
 
 
 def merge_in_kernel(got_refs, merged_ref, units):
@@ -193,7 +195,7 @@
             at = pair * segments + segment
             line = source_ref[holder, at : at + 1, :].astype(jnp.float32)
             moved = toeplitz_rows(
-                jnp.concatenate([line, spare], axis=1), sample_count + LANES
+                jnp.concatenate([line, spare], axis=1), sample_count + LANES, 1
             ).astype(jnp.bfloat16)
             padded = jnp.concatenate([edge, moved, edge], axis=1)
             rows = merged_ref[block, segment]
@@ -201,14 +203,12 @@
                 [rows[:, half * TILE : (half + 1) * TILE] for half in range(halves)], axis=0
             )
             for step in range(halves + 1):
-                low = step * TILE
+                low = sample_count - step * TILE
                 tile = jnp.concatenate(
                     [padded[:, low + LANES : low + LANES + TILE], padded[:, low : low + TILE]],
                     axis=0,
                 )
-                product = lax.dot_general(
-                    taken, tile, (((1,), (1,)), ((), ())), preferred_element_type=jnp.float32
-                )
+                product = jnp.dot(taken, tile, preferred_element_type=jnp.float32)
                 for half in range(halves):
                     lag_tile = half + MAX_LAG // TILE - step
                     part = product[half * owned : (half + 1) * owned]
@@ -245,7 +245,7 @@
         out_specs=pl.BlockSpec(memory_space=pltpu.VMEM),
         scratch_shapes=scratch,
         name="correlate",
-    )(source_channel, receiver_block, sources, *receivers)
+    )(source_channel, receiver_block, near_core(sources), *map(near_core, receivers))
 
 
 def local(recordings, gap_start, dropout_extent, filter_taps, source_channel, receiver_block):

time: 38.4 us -> 34.1 us (0.89); the launches traced: 37.7 us -> 33.8 us
  Pallas kernels: 11.5 us -> 7.12 us
  waiting for transfers between devices: 0.29 us -> 2.44 us
  blocking collectives: 23.9 us -> 23 us
  local copies, waits for them, and re-layouts: 0.71 us -> 0 us
    pallas_call x2, Pallas kernels: 7.19 us -> 3.82 us  [the longest x1 2.94 us: normalize(): pl.pallas_call(body, out_shape=pltpu.VMEM((slots, blocks * kept, sample_c...]
    ppermute x1, waiting for transfers between devices: 0.29 us -> 2.44 us  [local(): lax.ppermute(got, 'chan', [(group, group - 1) for group in range(1, group...]
    pallas_call x1, Pallas kernels: 4.28 us -> 3.3 us  [correlate(): pl.pallas_call(body, out_shape=jax.ShapeDtypeStruct((owned, pair_count, 2...]
    unnamed x4 -> x0, local copies, waits for them, and re-layouts: 0.71 us -> none
    all_gather x1, blocking collectives: 5.9 us -> 5.23 us  [local(): sources = lax.all_gather(picked, 'tm')]
  transfers between devices with their start and end apart: 1 -> 1, of which waited for: 1 -> 1; matrix products, arithmetic and copies ran while one was open for 0% -> 0% of each run, Pallas kernels for 6% -> 3%
where the time goes in v3:
time: 34.1 us; the launch traced here: 33.8 us
  blocking collectives  23 us (67%)
  Pallas kernels  7.12 us (21%)
  waiting for transfers between devices  2.44 us (7%)
  starting transfers between devices  1.28 us (4%)
    all_to_all x1, blocking collectives, local(): lax.all_to_all(sent.reshape(segments * groups, near * kept, sample_count)...  17.8 us
    all_gather x1, blocking collectives, local(): sources = lax.all_gather(picked, 'tm')  5.23 us
    pallas_call x1, Pallas kernels, correlate(): pl.pallas_call(body, out_shape=jax.ShapeDtypeStruct((owned, pair_count, 2...  3.3 us
    pallas_call x1, Pallas kernels, normalize(): pl.pallas_call(body, out_shape=pltpu.VMEM((slots, blocks * kept, sample_c...  2.94 us
    ppermute x1, waiting for transfers between devices, local(): lax.ppermute(got, 'chan', [(group, group - 1) for group in range(1, group...  2.44 us
    ppermute x1, starting transfers between devices, local(): lax.ppermute(got, 'chan', [(group, group - 1) for group in range(1, group...  1.28 us
    pallas_call x1, Pallas kernels, pick_sources(): pl.pallas_call(body, out_shape=pltpu.VMEM((count, got.shape[2]), jnp.bflo...  0.88 us
  transfers between devices with their start and end apart: 1, of which 1 were waited for; matrix products, arithmetic and copies ran while one was open for 0% of the time, Pallas kernels for 3%

profile of v3, /device:TPU:0, one launch (start us, length us, event | category | flops | bytes accessed | tf_op | source)
XLA Modules:
  0.0 33.8 jit_solution(14105836468292206827)
XLA Ops:
  0.0 2.9 %normalize.1 = bf16[4,64,512]{2,1,0:T(8,128)(2,1)S(1)} custom-call(f32[16,4,16,128]{3,2,1,0:T(8,128)} %bitcast.8, s32[1,256]{1,0:T(1,128)} %bitcast.9, s32[1,256]{1,0:T(1,128)} %bitcast.10, f32[1,128]{1,0:T(1,128)} %bitcast.11), custom_call_target="tpu_custom_call" | custom-call | tf_op jit(solution)/shard_map/normalize/pallas_call | solution.py:94
  2.9 17.8 %all_to_all.5.refs_1_.refs_3_ = bf16[32,8,512]{2,1,0:T(8,128)(2,1)S(1)} all-to-all(bf16[32,8,512]{2,1,0:T(8,128)(2,1)S(1)} %bitcast.6), channel_id=1, replica_groups=mesh['tm'=4,'chan'=8] {'tm','chan'}, dimensions={0} | all-to-all | bytes 524288 | tf_op jit(solution)/shard_map/all_to_all | solution.py:267
  20.7 1.3 %collective-permute-start = (bf16[32,8,512]{2,1,0:T(8,128)(2,1)S(1)}, bf16[32,8,512]{2,1,0:T(8,128)(2,1)S(1)}, u32[]{:S(2)}, u32[]{:S(2)}) collective-permute-start(bf16[32,8,512]{2,1,0:T(8,128)(2,1)S(1)} %all_to_all.5.refs_1_.refs_3_), channel_id=1, source_target_pairs={{1,0},{2,1},{3,2},{4,3},{5,4},{6,5},{7,6},{9,8},{10,9},{11,10},{12... | collective-permute-start | bytes 786440 | tf_op jit(solution)/shard_map/ppermute | solution.py:274
  22.0 0.9 %pick_sources.1 = bf16[16,512]{1,0:T(8,128)(2,1)S(1)} custom-call(s32[4]{0:T(128)} %refs_0_.3, bf16[32,8,512]{2,1,0:T(8,128)(2,1)S(1)} %all_to_all.5.refs_1_.refs_3_), custom_call_target="tpu_custom_call" | custom-call | tf_op jit(solution)/shard_map/pick_sources/pallas_call | solution.py:147
  22.9 5.2 %all-gather = bf16[64,512]{1,0:T(8,128)(2,1)S(1)} all-gather(bf16[16,512]{1,0:T(8,128)(2,1)S(1)} %pick_sources.1), channel_id=2, replica_groups=mesh['tm'=4,'chan'=8] {'tm'}, dimensions={0}, use_global_device_ids=true | all-gather | bytes 81920 | tf_op jit(solution)/shard_map/all_gather | solution.py:276
  28.1 2.4 %collective-permute-done.refs_4_ = bf16[32,8,512]{2,1,0:T(8,128)(2,1)S(1)} collective-permute-done((bf16[32,8,512]{2,1,0:T(8,128)(2,1)S(1)}, bf16[32,8,512]{2,1,0:T(8,128)(2,1)S(1)}, u32[]{:S(2)}, u32[]{:S(2)}) %collective-permute-start) | collective-permute-done | bytes 262176 | tf_op jit(solution)/shard_map/ppermute | solution.py:274
  30.5 3.3 %correlate.1 = f32[32,4,1024]{2,1,0:T(4,128)} custom-call(s32[4]{0:T(128)} %refs_0_.3, s32[4]{0:T(128)} %refs_1_.1, bf16[4,16,512]{2,1,0:T(8,128)(2,1)S(1)} %bitcast.7, bf16[32,8,512]{2,1,0:T(8,128)(2,1)S(1)} %all_to_all.5.refs_1_.refs_3_, bf16[32,8,512]{2,1,0:T(8,128)(2,1)S(1)} %collective-permute-done.refs_4_), custom_call_target="tpu_custom_call" | custom-call | tf_op jit(solution)/shard_map/correlate/pallas_call | solution.py:240
Async XLA Ops:
  20.7 9.8 %collective-permute-start = (bf16[32,8,512]{2,1,0:T(8,128)(2,1)S(1)}, bf16[32,8,512]{2,1,0:T(8,128)(2,1)S(1)}, u32[]{:S(2)}, u32[]{:S(2)}) collective-permute-start(bf16[32,8,512]{2,1,0:T(8,128)(2,1)S(1)} %all_to_all.5.refs_1_.refs_3_), channel_id=1, source_target_pairs={{1,0},{2,1},{3,2},{4,3},{5,4},{6,5},{7,6},{9,8},{10,9},{11,10},{12... | collective-permute-start | bytes 786440 | tf_op jit(solution)/shard_map/ppermute | solution.py:274

commit v4 on v3

--- a/solution.py
+++ b/solution.py
@@ -10,12 +10,16 @@
 BLOCK = 128
 MAX_LAG = 512
 LANES = 128
-TILE = 256
+KERNEL_VMEM = 24 << 20
 NEAR = 4
 
 
 def near_core(x):
     return pltpu.with_memory_space_constraint(x, pltpu.VMEM)
+
+
+def far(x):
+    return pltpu.with_memory_space_constraint(x, pltpu.HBM)
 
 
 def toeplitz_rows(row, width, first=0):
@@ -153,99 +157,167 @@
         ],
         out_specs=pl.BlockSpec(memory_space=pltpu.VMEM),
         name="pick_sources",
-    )(source_channel, near_core(got))
-
-
-def merge_in_kernel(got_refs, merged_ref, units):
-    segments = merged_ref.shape[1]
+    )(far(source_channel), near_core(got))
+
+
+def merge_in_kernel(got_ref, merged_ref, units):
     upper = lax.broadcasted_iota(jnp.int32, (8, merged_ref.shape[3]), 0) < 4
-    for group, got_ref in enumerate(got_refs):
-        for segment in range(segments):
-            for first in range(0, units, 4):
-                parts = [[], []]
-                for unit in (first, first + 2):
-                    a = got_ref[segment * units + unit].astype(jnp.float32)
-                    b = got_ref[segment * units + unit + 1].astype(jnp.float32)
-                    parts[0].append(jnp.where(upper, a, pltpu.roll(b, 4, 0)))
-                    parts[1].append(jnp.where(upper, pltpu.roll(a, 4, 0), b))
-                for block in range(2):
-                    merged_ref[2 * group + block, segment, first * 4 : first * 4 + 16, :] = (
-                        jnp.concatenate(parts[block], axis=0).astype(jnp.bfloat16)
-                    )
-
-
-def correlate_kernel(owned, kept, units, merged_here, channel_ref, block_ref, source_ref, *refs):
+    for segment in range(merged_ref.shape[1]):
+        for first in range(0, units, 4):
+            parts = [[], []]
+            for unit in (first, first + 2):
+                a = got_ref[segment * units + unit].astype(jnp.float32)
+                b = got_ref[segment * units + unit + 1].astype(jnp.float32)
+                parts[0].append(jnp.where(upper, a, pltpu.roll(b, 4, 0)))
+                parts[1].append(jnp.where(upper, pltpu.roll(a, 4, 0), b))
+            for block in range(2):
+                merged_ref[block, segment, first * 4 : first * 4 + 16, :] = jnp.concatenate(
+                    parts[block], axis=0
+                ).astype(jnp.bfloat16)
+
+
+def prepare_kernel(owned, units, merged_here, channel_ref, source_ref, *refs):
     if merged_here:
-        own_ref, next_ref, out_ref, lines_ref, merged_ref = refs
-        merge_in_kernel((own_ref, next_ref), merged_ref, units)
+        own_ref, moved_ref, merged_ref = refs
+        merge_in_kernel(own_ref, merged_ref, units)
     else:
-        merged_ref, out_ref, lines_ref = refs
-    segments, _, sample_count = merged_ref.shape[1:]
+        (moved_ref,) = refs
     pair_count = channel_ref.shape[0]
-    factor = 1.0 / math.sqrt(sample_count * segments)
-    halves = sample_count // TILE
-    lag_tiles = 2 * MAX_LAG // TILE
+    segments = source_ref.shape[1] // pair_count
     spare = jnp.zeros((1, LANES), jnp.float32)
-    edge = jnp.zeros((LANES, LANES), jnp.bfloat16)
     for pair in range(pair_count):
         holder = (channel_ref[pair] % BLOCK) // owned
-        block = block_ref[pair]
-        sums = [None] * lag_tiles
         for segment in range(segments):
             at = pair * segments + segment
             line = source_ref[holder, at : at + 1, :].astype(jnp.float32)
-            moved = toeplitz_rows(
-                jnp.concatenate([line, spare], axis=1), sample_count + LANES, 1
-            ).astype(jnp.bfloat16)
-            padded = jnp.concatenate([edge, moved, edge], axis=1)
-            rows = merged_ref[block, segment]
-            taken = jnp.concatenate(
-                [rows[:, half * TILE : (half + 1) * TILE] for half in range(halves)], axis=0
-            )
-            for step in range(halves + 1):
-                low = sample_count - step * TILE
-                tile = jnp.concatenate(
-                    [padded[:, low + LANES : low + LANES + TILE], padded[:, low : low + TILE]],
-                    axis=0,
+            line = jnp.concatenate([line, spare], axis=1)
+            moved_ref[at] = toeplitz_rows(line, line.shape[1], 1).astype(jnp.bfloat16)
+
+
+def prepare(source_channel, sources, own, owned, units):
+    pair_count = source_channel.shape[0]
+    count, sample_count = sources.shape[1:]
+    out_shape = [pltpu.VMEM((count, LANES, sample_count + LANES), jnp.bfloat16)]
+    if own:
+        merged = (NEAR // 2, count // pair_count, owned, sample_count)
+        out_shape.append(pltpu.VMEM(merged, jnp.bfloat16))
+
+    def body(*refs):
+        prepare_kernel(owned, units, bool(own), *refs)
+
+    return pl.pallas_call(
+        body,
+        out_shape=out_shape,
+        in_specs=[pl.BlockSpec(memory_space=pltpu.SMEM)]
+        + [pl.BlockSpec(memory_space=pltpu.VMEM)] * (1 + len(own)),
+        out_specs=[pl.BlockSpec(memory_space=pltpu.VMEM)] * len(out_shape),
+        compiler_params=pltpu.CompilerParams(vmem_limit_bytes=KERNEL_VMEM),
+        name="prepare",
+    )(far(source_channel), near_core(sources), *map(near_core, own))
+
+
+def lag_products(receivers, toeplitz):
+    rows, sample_count = receivers[0].shape
+    pieces = sample_count // LANES
+    empty = jnp.zeros((rows, LANES), receivers[0].dtype)
+    sides = []
+    stacked = []
+    pairs = []
+    last = []
+    for row, moved in zip(receivers, toeplitz, strict=True):
+        parts = [row[:, i * LANES : (i + 1) * LANES] for i in range(pieces)]
+        tiles = [
+            moved[:, (pieces - i) * LANES : (pieces - i + 1) * LANES] for i in range(pieces + 1)
+        ]
+        sides.append(jnp.concatenate([empty, *parts], axis=0))
+        sides.append(jnp.concatenate([*parts, empty], axis=0))
+        stacked.append(jnp.concatenate(parts, axis=0))
+        pairs.append(jnp.concatenate(tiles[0:pieces:2], axis=1))
+        pairs.append(jnp.concatenate(tiles[1:pieces:2], axis=1))
+        last.append(tiles[pieces])
+    first = jnp.dot(
+        jnp.concatenate(sides, axis=1),
+        jnp.concatenate(pairs, axis=0),
+        preferred_element_type=jnp.float32,
+    )
+    second = jnp.dot(
+        jnp.concatenate(stacked, axis=1),
+        jnp.concatenate(last, axis=0),
+        preferred_element_type=jnp.float32,
+    )
+    sums = [None] * (2 * pieces)
+    for i in range(pieces):
+        sums[i] = second[i * rows : (i + 1) * rows]
+    for column in range(pieces // 2):
+        for i in range(pieces + 1):
+            part = first[i * rows : (i + 1) * rows, column * LANES : (column + 1) * LANES]
+            chunk = i - 1 + pieces - 2 * column
+            sums[chunk] = part if sums[chunk] is None else sums[chunk] + part
+    return sums
+
+
+def correlate_kernel(owned, kept, units, merged_here, block_ref, moved_ref, *refs):
+    if merged_here:
+        own_ref, next_ref, out_hbm, lines_ref, out_ref, sems, after_ref = refs
+        merge_in_kernel(next_ref, after_ref, units)
+        segments, _, sample_count = own_ref.shape[1:]
+    else:
+        merged_ref, out_hbm, lines_ref, out_ref, sems = refs
+        segments, _, sample_count = merged_ref.shape[1:]
+    pair_count = block_ref.shape[0]
+    factor = 1.0 / math.sqrt(sample_count * segments)
+    across = owned // kept
+    copies = []
+    for pair in range(pair_count):
+        block = block_ref[pair]
+        if merged_here:
+            ahead = block >= NEAR // 2
+            place = block % (NEAR // 2)
+            receivers = [
+                jnp.where(ahead, after_ref[place, i], own_ref[place, i]) for i in range(segments)
+            ]
+        else:
+            receivers = [merged_ref[block, i] for i in range(segments)]
+        sums = lag_products(receivers, [moved_ref[pair * segments + i] for i in range(segments)])
+        for chunk, part in enumerate(sums):
+            lines_ref[chunk] = part * factor
+            low = chunk * LANES
+            for place in range(kept):
+                out_ref[place * across : (place + 1) * across, pair, low : low + LANES] = (
+                    lines_ref[chunk, pl.ds(place, across, stride=kept), :]
                 )
-                product = jnp.dot(taken, tile, preferred_element_type=jnp.float32)
-                for half in range(halves):
-                    lag_tile = half + MAX_LAG // TILE - step
-                    part = product[half * owned : (half + 1) * owned]
-                    old = sums[lag_tile]
-                    sums[lag_tile] = part if old is None else old + part
-        across = owned // kept
-        for lag_tile in range(lag_tiles):
-            for part in range(TILE // LANES):
-                low = part * LANES
-                lines_ref[...] = sums[lag_tile][:, low : low + LANES] * factor
-                low = low + lag_tile * TILE
-                for place in range(kept):
-                    out_ref[place * across : (place + 1) * across, pair, low : low + LANES] = (
-                        lines_ref[pl.ds(place, across, stride=kept), :]
-                    )
-
-
-def correlate(source_channel, receiver_block, sources, receivers, owned, kept, units):
-    pair_count = source_channel.shape[0]
-    segments, sample_count = sources.shape[1] // pair_count, sources.shape[2]
+        copy = pltpu.make_async_copy(out_ref.at[:, pair], out_hbm.at[:, pair], sems.at[pair])
+        copy.start()
+        copies.append(copy)
+    for copy in copies:
+        copy.wait()
+
+
+def correlate(receiver_block, toeplitz, receivers, owned, kept, units):
+    pair_count = receiver_block.shape[0]
     merged_here = len(receivers) == 2
+    shape = (owned, pair_count, 2 * MAX_LAG)
 
     def body(*refs):
         correlate_kernel(owned, kept, units, merged_here, *refs)
 
-    scratch = [pltpu.VMEM((owned, LANES), jnp.float32)]
+    scratch = [
+        pltpu.VMEM((2 * MAX_LAG // LANES, owned, LANES), jnp.float32),
+        pltpu.VMEM(shape, jnp.float32),
+        pltpu.SemaphoreType.DMA((pair_count,)),
+    ]
     if merged_here:
-        scratch.append(pltpu.VMEM((NEAR, segments, owned, sample_count), jnp.bfloat16))
+        scratch.append(pltpu.VMEM(receivers[0].shape, jnp.bfloat16))
     return pl.pallas_call(
         body,
-        out_shape=jax.ShapeDtypeStruct((owned, pair_count, 2 * MAX_LAG), jnp.float32),
-        in_specs=[pl.BlockSpec(memory_space=pltpu.SMEM)] * 2
+        out_shape=jax.ShapeDtypeStruct(shape, jnp.float32),
+        in_specs=[pl.BlockSpec(memory_space=pltpu.SMEM)]
         + [pl.BlockSpec(memory_space=pltpu.VMEM)] * (1 + len(receivers)),
-        out_specs=pl.BlockSpec(memory_space=pltpu.VMEM),
+        out_specs=pl.BlockSpec(memory_space=pl.ANY),
         scratch_shapes=scratch,
+        compiler_params=pltpu.CompilerParams(vmem_limit_bytes=KERNEL_VMEM),
         name="correlate",
-    )(source_channel, receiver_block, near_core(sources), *map(near_core, receivers))
+    )(far(receiver_block), near_core(toeplitz), *map(near_core, receivers))
 
 
 def local(recordings, gap_start, dropout_extent, filter_taps, source_channel, receiver_block):
@@ -274,16 +346,16 @@
     following = lax.ppermute(got, "chan", [(group, group - 1) for group in range(1, groups)])
     picked = pick_sources(source_channel, got, units, kept, segments)
     sources = lax.all_gather(picked, "tm")
-    receivers = (got, following)
-    if kept != 4 or owned != 4 * units or near != 2:
-        across = owned // kept
-        first = lax.axis_index("tm") * owned % units
-        apart = [x.reshape(segments, units, near, kept, sample_count) for x in receivers]
-        apart = lax.dynamic_slice_in_dim(jnp.concatenate(apart, axis=2), first, across, axis=1)
-        receivers = (
-            apart.transpose(2, 0, 1, 3, 4).reshape(2 * near, segments, owned, sample_count),
-        )
-    return correlate(source_channel, receiver_block, sources, receivers, owned, kept, units)
+    if kept == 4 and owned == 4 * units and near == 2:
+        toeplitz, own = prepare(source_channel, sources, (got,), owned, units)
+        return correlate(receiver_block, toeplitz, (own, following), owned, kept, units)
+    across = owned // kept
+    first = lax.axis_index("tm") * owned % units
+    apart = [x.reshape(segments, units, near, kept, sample_count) for x in (got, following)]
+    apart = lax.dynamic_slice_in_dim(jnp.concatenate(apart, axis=2), first, across, axis=1)
+    merged = apart.transpose(2, 0, 1, 3, 4).reshape(2 * near, segments, owned, sample_count)
+    (toeplitz,) = prepare(source_channel, sources, (), owned, units)
+    return correlate(receiver_block, toeplitz, (merged,), owned, kept, units)
 
 
 def solution(mesh):

time: 34.1 us -> 33.2 us (0.974)
  waiting for transfers between devices: 2.44 us -> 1.03 us
  Pallas kernels: 7.12 us -> 7.66 us
    ppermute x1, waiting for transfers between devices: 2.44 us -> 1.03 us  [local(): lax.ppermute(got, 'chan', [(group, group - 1) for group in range(1, group...]
    pallas_call x1 -> x2, Pallas kernels: 3.3 us -> 3.84 us  [the longest x1 2.44 us: correlate(): pl.pallas_call(body, out_shape=jax.ShapeDtypeStruct(shape, jnp.float32),...]
  transfers between devices with their start and end apart: 1 -> 1, of which waited for: 1 -> 1; matrix products, arithmetic and copies ran while one was open for 0% -> 0% of each run, Pallas kernels for 3% -> 7%
where the time goes in v4:
time: 33.2 us; the launch traced here: 33 us
  blocking collectives  23 us (69%)
  Pallas kernels  7.66 us (23%)
  starting transfers between devices  1.28 us (4%)
  waiting for transfers between devices  1.03 us (3%)
    all_to_all x1, blocking collectives, local(): lax.all_to_all(sent.reshape(segments * groups, near * kept, sample_count)...  17.8 us
    all_gather x1, blocking collectives, local(): sources = lax.all_gather(picked, 'tm')  5.23 us
    pallas_call x1, Pallas kernels, normalize(): pl.pallas_call(body, out_shape=pltpu.VMEM((slots, blocks * kept, sample_c...  2.94 us
    pallas_call x1, Pallas kernels, correlate(): pl.pallas_call(body, out_shape=jax.ShapeDtypeStruct(shape, jnp.float32),...  2.44 us
    pallas_call x1, Pallas kernels, prepare(): pl.pallas_call(body, out_shape=out_shape, in_specs=[pl.BlockSpec(memory_s...  1.4 us
    ppermute x1, starting transfers between devices, local(): lax.ppermute(got, 'chan', [(group, group - 1) for group in range(1, group...  1.28 us
    ppermute x1, waiting for transfers between devices, local(): lax.ppermute(got, 'chan', [(group, group - 1) for group in range(1, group...  1.03 us
    pallas_call x1, Pallas kernels, pick_sources(): pl.pallas_call(body, out_shape=pltpu.VMEM((count, got.shape[2]), jnp.bflo...  0.88 us
  transfers between devices with their start and end apart: 1, of which 1 were waited for; matrix products, arithmetic and copies ran while one was open for 0% of the time, Pallas kernels for 7%

profile of v4, /device:TPU:0, one launch (start us, length us, event | category | flops | bytes accessed | tf_op | source)
XLA Modules:
  0.0 33.0 jit_solution(1415010522554363849)
XLA Ops:
  0.0 2.9 %normalize.1 = bf16[4,64,512]{2,1,0:T(8,128)(2,1)S(1)} custom-call(f32[16,4,16,128]{3,2,1,0:T(8,128)} %bitcast.8, s32[1,256]{1,0:T(1,128)} %bitcast.9, s32[1,256]{1,0:T(1,128)} %bitcast.10, f32[1,128]{1,0:T(1,128)} %bitcast.11), custom_call_target="tpu_custom_call" | custom-call | tf_op jit(solution)/shard_map/normalize/pallas_call | solution.py:98
  2.9 17.8 %all_to_all.5.refs_1_.refs_2_ = bf16[32,8,512]{2,1,0:T(8,128)(2,1)S(1)} all-to-all(bf16[32,8,512]{2,1,0:T(8,128)(2,1)S(1)} %bitcast.6), channel_id=1, replica_groups=mesh['tm'=4,'chan'=8] {'tm','chan'}, dimensions={0} | all-to-all | bytes 524288 | tf_op jit(solution)/shard_map/all_to_all | solution.py:339
  20.7 1.3 %collective-permute-start = (bf16[32,8,512]{2,1,0:T(8,128)(2,1)S(1)}, bf16[32,8,512]{2,1,0:T(8,128)(2,1)S(1)}, u32[]{:S(2)}, u32[]{:S(2)}) collective-permute-start(bf16[32,8,512]{2,1,0:T(8,128)(2,1)S(1)} %all_to_all.5.refs_1_.refs_2_), channel_id=1, source_target_pairs={{1,0},{2,1},{3,2},{4,3},{5,4},{6,5},{7,6},{9,8},{10,9},{11,10},{12... | collective-permute-start | bytes 786440 | tf_op jit(solution)/shard_map/ppermute | solution.py:346
  22.0 0.9 %pick_sources.1 = bf16[16,512]{1,0:T(8,128)(2,1)S(1)} custom-call(s32[4]{0:T(128)} %refs_0_.4, bf16[32,8,512]{2,1,0:T(8,128)(2,1)S(1)} %all_to_all.5.refs_1_.refs_2_), custom_call_target="tpu_custom_call" | custom-call | tf_op jit(solution)/shard_map/pick_sources/pallas_call | solution.py:151
  22.9 5.2 %all-gather = bf16[64,512]{1,0:T(8,128)(2,1)S(1)} all-gather(bf16[16,512]{1,0:T(8,128)(2,1)S(1)} %pick_sources.1), channel_id=2, replica_groups=mesh['tm'=4,'chan'=8] {'tm'}, dimensions={0}, use_global_device_ids=true | all-gather | bytes 81920 | tf_op jit(solution)/shard_map/all_gather | solution.py:348
  28.1 1.4 %prepare.1 = (bf16[16,128,640]{2,1,0:T(8,128)(2,1)S(1)}, bf16[2,4,32,512]{3,2,1,0:T(8,128)(2,1)S(1)}) custom-call(s32[4]{0:T(128)} %refs_0_.4, bf16[4,16,512]{2,1,0:T(8,128)(2,1)S(1)} %bitcast.7, bf16[32,8,512]{2,1,0:T(8,128)(2,1)S(1)} %all_to_all.5.refs_1_.refs_2_), custom_call_target="tpu_custom_call" | custom-call | tf_op jit(solution)/shard_map/prepare/pallas_call | solution.py:208
  29.5 1.0 %collective-permute-done.refs_3_ = bf16[32,8,512]{2,1,0:T(8,128)(2,1)S(1)} collective-permute-done((bf16[32,8,512]{2,1,0:T(8,128)(2,1)S(1)}, bf16[32,8,512]{2,1,0:T(8,128)(2,1)S(1)}, u32[]{:S(2)}, u32[]{:S(2)}) %collective-permute-start) | collective-permute-done | bytes 262176 | tf_op jit(solution)/shard_map/ppermute | solution.py:346
  30.5 2.4 %correlate.1 = f32[32,4,1024]{2,1,0:T(4,128)} custom-call(s32[4]{0:T(128)} %refs_0_.5, bf16[16,128,640]{2,1,0:T(8,128)(2,1)S(1)} %get-tuple-element.7.refs_1_, bf16[2,4,32,512]{3,2,1,0:T(8,128)(2,1)S(1)} %get-tuple-element.8.refs_2_, bf16[32,8,512]{2,1,0:T(8,128)(2,1)S(1)} %collective-permute-done.refs_3_), custom_call_target="tpu_custom_call" | custom-call | tf_op jit(solution)/shard_map/correlate/pallas_call | solution.py:311
Async XLA Ops:
  20.7 9.8 %collective-permute-start = (bf16[32,8,512]{2,1,0:T(8,128)(2,1)S(1)}, bf16[32,8,512]{2,1,0:T(8,128)(2,1)S(1)}, u32[]{:S(2)}, u32[]{:S(2)}) collective-permute-start(bf16[32,8,512]{2,1,0:T(8,128)(2,1)S(1)} %all_to_all.5.refs_1_.refs_2_), channel_id=1, source_target_pairs={{1,0},{2,1},{3,2},{4,3},{5,4},{6,5},{7,6},{9,8},{10,9},{11,10},{12... | collective-permute-start | bytes 786440 | tf_op jit(solution)/shard_map/ppermute | solution.py:346

commit v5 on v4

--- a/solution.py
+++ b/solution.py
@@ -9,6 +9,7 @@
 
 BLOCK = 128
 MAX_LAG = 512
+PAIR_DEV = 4
 LANES = 128
 KERNEL_VMEM = 24 << 20
 NEAR = 4
@@ -18,32 +19,52 @@
     return pltpu.with_memory_space_constraint(x, pltpu.VMEM)
 
 
-def far(x):
-    return pltpu.with_memory_space_constraint(x, pltpu.HBM)
-
-
 def toeplitz_rows(row, width, first=0):
     return pltpu.roll(
         jnp.broadcast_to(row, (LANES, width)), first, 1, stride=1, stride_axis=0
     )
 
 
-def normalize_kernel(
-    slots, kept, rec_hbm, start_ref, extent_ref, taps_ref, out_ref, rec_ref, sems
-):
+def in_parts(x):
+    first = x.astype(jnp.bfloat16)
+    rest = x - first.astype(jnp.float32)
+    second = rest.astype(jnp.bfloat16)
+    return first, second, (rest - second.astype(jnp.float32)).astype(jnp.bfloat16)
+
+
+def normalize_kernel(slots, kept, rec_hbm, *refs):
+    small_refs, (out_ref, index_ref, rec_ref), small_bufs, sems = (
+        refs[:5],
+        refs[5:8],
+        refs[8:13],
+        refs[13],
+    )
     blocks = rec_hbm.shape[0]
     rows = blocks * kept
     pieces = rec_hbm.shape[2] // kept
     sample_count = pieces * LANES
+    small = []
+    for i, (small_ref, small_buf) in enumerate(zip(small_refs, small_bufs, strict=True)):
+        copy = pltpu.make_async_copy(small_ref, small_buf, sems.at[slots + i])
+        copy.start()
+        small.append(copy)
     copies = []
     for slot in range(slots):
         copy = pltpu.make_async_copy(rec_hbm.at[:, slot], rec_ref.at[slot], sems.at[slot])
         copy.start()
         copies.append(copy)
+    for copy in small:
+        copy.wait()
+    taps_ref, start_ref, extent_ref, channel_ref, block_ref = small_bufs
     taps = jnp.concatenate([taps_ref[...], jnp.zeros((1, LANES), jnp.float32)], axis=1)
-    weights = toeplitz_rows(taps, 2 * LANES)
+    w0, w1, w2 = in_parts(toeplitz_rows(taps, 2 * LANES))
+    weights = jnp.concatenate([w0, w0, w0, w1, w1, w2], axis=0)
     starts = start_ref[...].astype(jnp.float32)
     ends = starts + extent_ref[...].astype(jnp.float32)
+    for i, ref in enumerate((channel_ref, block_ref)):
+        for pair in range(PAIR_DEV):
+            value = jnp.broadcast_to(ref[:, pair : pair + 1], (1, LANES))
+            index_ref[i * PAIR_DEV + pair : i * PAIR_DEV + pair + 1, :] = value
     round_count = starts.shape[1]
     lane = lax.broadcasted_iota(jnp.int32, (rows, round_count), 1)
     row = lax.broadcasted_iota(jnp.int32, (rows, round_count), 0)
@@ -66,11 +87,11 @@
             valid = jnp.where((at >= start) & (at < end), 0.0, 1.0)
             valids.append(valid)
             masked.append(flat[pl.ds(piece, rows, stride=pieces), :] * valid)
+        x0, x1, x2 = in_parts(jnp.concatenate(masked, axis=0))
         spread = jnp.dot(
-            jnp.concatenate(masked, axis=0),
+            jnp.concatenate([x0, x1, x2, x0, x1, x0], axis=1),
             weights,
             preferred_element_type=jnp.float32,
-            precision=lax.Precision.HIGHEST,
         )
         kept_parts = []
         squares = jnp.zeros((rows, LANES), jnp.float32)
@@ -87,8 +108,8 @@
         out_ref[slot] = normalized.astype(out_ref.dtype)
 
 
-def normalize(recordings, gap_start, dropout_extent, filter_taps, blocks, slots, kept):
-    round_count, sample_count = recordings.shape[1], recordings.shape[3]
+def normalize(recordings, small, blocks, slots, kept):
+    sample_count = recordings.shape[3]
     pieces = sample_count // LANES
     view = recordings.reshape(blocks, slots, kept * pieces, LANES)
 
@@ -97,34 +118,32 @@
 
     return pl.pallas_call(
         body,
-        out_shape=pltpu.VMEM((slots, blocks * kept, sample_count), jnp.bfloat16),
-        in_specs=[
-            pl.BlockSpec(memory_space=pl.ANY),
-            pl.BlockSpec(memory_space=pltpu.VMEM),
-            pl.BlockSpec(memory_space=pltpu.VMEM),
-            pl.BlockSpec(memory_space=pltpu.VMEM),
-        ],
-        out_specs=pl.BlockSpec(memory_space=pltpu.VMEM),
+        out_shape=(
+            pltpu.VMEM((slots, blocks * kept, sample_count), jnp.bfloat16),
+            pltpu.VMEM((2 * PAIR_DEV, LANES), jnp.int32),
+        ),
+        in_specs=[pl.BlockSpec(memory_space=pl.ANY)] * (1 + len(small)),
+        out_specs=[pl.BlockSpec(memory_space=pltpu.VMEM)] * 2,
         scratch_shapes=[
             pltpu.VMEM((slots, blocks, kept * pieces, LANES), jnp.float32),
-            pltpu.SemaphoreType.DMA((slots,)),
+            *[pltpu.VMEM(x.shape, x.dtype) for x in small],
+            pltpu.SemaphoreType.DMA((slots + len(small),)),
         ],
         name="normalize",
-    )(
-        view,
-        gap_start.reshape(1, round_count),
-        dropout_extent.reshape(1, round_count),
-        filter_taps.reshape(1, LANES),
-    )
-
-
-def pick_kernel(units, kept, segments, channel_ref, got_ref, out_ref):
+    )(view, *small)
+
+
+def index_at(index_ref, row):
+    return jnp.max(index_ref[row : row + 1, :].astype(jnp.float32)).astype(jnp.int32)
+
+
+def pick_kernel(units, kept, segments, index_ref, got_ref, out_ref):
     sample_count = got_ref.shape[2]
     shape = got_ref.shape[1:]
     row = lax.broadcasted_iota(jnp.int32, shape, 0)
     found = []
-    for pair in range(channel_ref.shape[0]):
-        channel = channel_ref[pair]
+    for pair in range(PAIR_DEV):
+        channel = index_at(index_ref, pair)
         unit = channel % units
         wanted = row == (channel // BLOCK) * kept + ((channel % BLOCK) // units) % kept
         for segment in range(segments):
@@ -142,8 +161,8 @@
         ).astype(out_ref.dtype)
 
 
-def pick_sources(source_channel, got, units, kept, segments):
-    count = source_channel.shape[0] * segments
+def pick_sources(index, got, units, kept, segments):
+    count = PAIR_DEV * segments
 
     def body(*refs):
         pick_kernel(units, kept, segments, *refs)
@@ -152,12 +171,12 @@
         body,
         out_shape=pltpu.VMEM((count, got.shape[2]), jnp.bfloat16),
         in_specs=[
-            pl.BlockSpec(memory_space=pltpu.SMEM),
+            pl.BlockSpec(memory_space=pltpu.VMEM),
             pl.BlockSpec(memory_space=pltpu.VMEM),
         ],
         out_specs=pl.BlockSpec(memory_space=pltpu.VMEM),
         name="pick_sources",
-    )(far(source_channel), near_core(got))
+    )(near_core(index), near_core(got))
 
 
 def merge_in_kernel(got_ref, merged_ref, units):
@@ -176,17 +195,16 @@
                 ).astype(jnp.bfloat16)
 
 
-def prepare_kernel(owned, units, merged_here, channel_ref, source_ref, *refs):
+def prepare_kernel(owned, units, merged_here, index_ref, source_ref, *refs):
     if merged_here:
         own_ref, moved_ref, merged_ref = refs
         merge_in_kernel(own_ref, merged_ref, units)
     else:
         (moved_ref,) = refs
-    pair_count = channel_ref.shape[0]
-    segments = source_ref.shape[1] // pair_count
+    segments = source_ref.shape[1] // PAIR_DEV
     spare = jnp.zeros((1, LANES), jnp.float32)
-    for pair in range(pair_count):
-        holder = (channel_ref[pair] % BLOCK) // owned
+    for pair in range(PAIR_DEV):
+        holder = (index_at(index_ref, pair) % BLOCK) // owned
         for segment in range(segments):
             at = pair * segments + segment
             line = source_ref[holder, at : at + 1, :].astype(jnp.float32)
@@ -194,12 +212,11 @@
             moved_ref[at] = toeplitz_rows(line, line.shape[1], 1).astype(jnp.bfloat16)
 
 
-def prepare(source_channel, sources, own, owned, units):
-    pair_count = source_channel.shape[0]
+def prepare(index, sources, own, owned, units):
     count, sample_count = sources.shape[1:]
     out_shape = [pltpu.VMEM((count, LANES, sample_count + LANES), jnp.bfloat16)]
     if own:
-        merged = (NEAR // 2, count // pair_count, owned, sample_count)
+        merged = (NEAR // 2, count // PAIR_DEV, owned, sample_count)
         out_shape.append(pltpu.VMEM(merged, jnp.bfloat16))
 
     def body(*refs):
@@ -208,12 +225,11 @@
     return pl.pallas_call(
         body,
         out_shape=out_shape,
-        in_specs=[pl.BlockSpec(memory_space=pltpu.SMEM)]
-        + [pl.BlockSpec(memory_space=pltpu.VMEM)] * (1 + len(own)),
+        in_specs=[pl.BlockSpec(memory_space=pltpu.VMEM)] * (2 + len(own)),
         out_specs=[pl.BlockSpec(memory_space=pltpu.VMEM)] * len(out_shape),
         compiler_params=pltpu.CompilerParams(vmem_limit_bytes=KERNEL_VMEM),
         name="prepare",
-    )(far(source_channel), near_core(sources), *map(near_core, own))
+    )(near_core(index), near_core(sources), *map(near_core, own))
 
 
 def lag_products(receivers, toeplitz):
@@ -256,7 +272,7 @@
     return sums
 
 
-def correlate_kernel(owned, kept, units, merged_here, block_ref, moved_ref, *refs):
+def correlate_kernel(owned, kept, units, merged_here, index_ref, moved_ref, *refs):
     if merged_here:
         own_ref, next_ref, out_hbm, lines_ref, out_ref, sems, after_ref = refs
         merge_in_kernel(next_ref, after_ref, units)
@@ -264,12 +280,11 @@
     else:
         merged_ref, out_hbm, lines_ref, out_ref, sems = refs
         segments, _, sample_count = merged_ref.shape[1:]
-    pair_count = block_ref.shape[0]
     factor = 1.0 / math.sqrt(sample_count * segments)
     across = owned // kept
     copies = []
-    for pair in range(pair_count):
-        block = block_ref[pair]
+    for pair in range(PAIR_DEV):
+        block = index_at(index_ref, PAIR_DEV + pair)
         if merged_here:
             ahead = block >= NEAR // 2
             place = block % (NEAR // 2)
@@ -293,10 +308,9 @@
         copy.wait()
 
 
-def correlate(receiver_block, toeplitz, receivers, owned, kept, units):
-    pair_count = receiver_block.shape[0]
+def correlate(index, toeplitz, receivers, owned, kept, units):
     merged_here = len(receivers) == 2
-    shape = (owned, pair_count, 2 * MAX_LAG)
+    shape = (owned, PAIR_DEV, 2 * MAX_LAG)
 
     def body(*refs):
         correlate_kernel(owned, kept, units, merged_here, *refs)
@@ -304,20 +318,19 @@
     scratch = [
         pltpu.VMEM((2 * MAX_LAG // LANES, owned, LANES), jnp.float32),
         pltpu.VMEM(shape, jnp.float32),
-        pltpu.SemaphoreType.DMA((pair_count,)),
+        pltpu.SemaphoreType.DMA((PAIR_DEV,)),
     ]
     if merged_here:
         scratch.append(pltpu.VMEM(receivers[0].shape, jnp.bfloat16))
     return pl.pallas_call(
         body,
         out_shape=jax.ShapeDtypeStruct(shape, jnp.float32),
-        in_specs=[pl.BlockSpec(memory_space=pltpu.SMEM)]
-        + [pl.BlockSpec(memory_space=pltpu.VMEM)] * (1 + len(receivers)),
+        in_specs=[pl.BlockSpec(memory_space=pltpu.VMEM)] * (2 + len(receivers)),
         out_specs=pl.BlockSpec(memory_space=pl.ANY),
         scratch_shapes=scratch,
         compiler_params=pltpu.CompilerParams(vmem_limit_bytes=KERNEL_VMEM),
         name="correlate",
-    )(far(receiver_block), near_core(toeplitz), *map(near_core, receivers))
+    )(near_core(index), near_core(toeplitz), *map(near_core, receivers))
 
 
 def local(recordings, gap_start, dropout_extent, filter_taps, source_channel, receiver_block):
@@ -331,9 +344,11 @@
     rounds_block = BLOCK // units
     slots = min(segments, rounds_block)
     kept = rounds_block // slots
-    normalized = normalize(
-        recordings, gap_start, dropout_extent, filter_taps, blocks, slots, kept
-    )
+    small = [
+        x.reshape(1, x.size)
+        for x in (filter_taps, gap_start, dropout_extent, source_channel, receiver_block)
+    ]
+    normalized, index = normalize(recordings, small, blocks, slots, kept)
     sent = normalized.reshape(slots, groups, near * kept, sample_count)
     sent = jnp.repeat(sent, segments // slots, axis=0) if segments > slots else sent
     got = lax.all_to_all(
@@ -344,18 +359,18 @@
         tiled=True,
     )
     following = lax.ppermute(got, "chan", [(group, group - 1) for group in range(1, groups)])
-    picked = pick_sources(source_channel, got, units, kept, segments)
+    picked = pick_sources(index, got, units, kept, segments)
     sources = lax.all_gather(picked, "tm")
     if kept == 4 and owned == 4 * units and near == 2:
-        toeplitz, own = prepare(source_channel, sources, (got,), owned, units)
-        return correlate(receiver_block, toeplitz, (own, following), owned, kept, units)
+        toeplitz, own = prepare(index, sources, (got,), owned, units)
+        return correlate(index, toeplitz, (own, following), owned, kept, units)
     across = owned // kept
     first = lax.axis_index("tm") * owned % units
     apart = [x.reshape(segments, units, near, kept, sample_count) for x in (got, following)]
     apart = lax.dynamic_slice_in_dim(jnp.concatenate(apart, axis=2), first, across, axis=1)
     merged = apart.transpose(2, 0, 1, 3, 4).reshape(2 * near, segments, owned, sample_count)
-    (toeplitz,) = prepare(source_channel, sources, (), owned, units)
-    return correlate(receiver_block, toeplitz, (merged,), owned, kept, units)
+    (toeplitz,) = prepare(index, sources, (), owned, units)
+    return correlate(index, toeplitz, (merged,), owned, kept, units)
 
 
 def solution(mesh):

time: 33.2 us -> 31.6 us (0.952)
  Pallas kernels: 7.66 us -> 5.4 us
  waiting for transfers between devices: 1.03 us -> 1.73 us
    pallas_call x1, Pallas kernels: 2.94 us -> 1.95 us  [normalize(): pl.pallas_call(body, out_shape=(pltpu.VMEM((slots, blocks * kept, sample_...]
    ppermute x1, waiting for transfers between devices: 1.03 us -> 1.73 us  [local(): lax.ppermute(got, 'chan', [(group, group - 1) for group in range(1, group...]
    pallas_call x1, Pallas kernels: 2.44 us -> 1.86 us  [correlate(): pl.pallas_call(body, out_shape=jax.ShapeDtypeStruct(shape, jnp.float32),...]
    pallas_call x1, Pallas kernels: 0.88 us -> 0.33 us  [pick_sources(): pl.pallas_call(body, out_shape=pltpu.VMEM((count, got.shape[2]), jnp.bflo...]
  transfers between devices with their start and end apart: 1 -> 1, of which waited for: 1 -> 1; matrix products, arithmetic and copies ran while one was open for 0% -> 0% of each run, Pallas kernels for 7% -> 5%
where the time goes in v5:
time: 31.6 us; the launch traced here: 31.4 us
  blocking collectives  23 us (73%)
  Pallas kernels  5.4 us (17%)
  waiting for transfers between devices  1.73 us (5%)
  starting transfers between devices  1.28 us (4%)
    all_to_all x1, blocking collectives, local(): lax.all_to_all(sent.reshape(segments * groups, near * kept, sample_count)...  17.8 us
    all_gather x1, blocking collectives, local(): sources = lax.all_gather(picked, 'tm')  5.23 us
    pallas_call x1, Pallas kernels, normalize(): pl.pallas_call(body, out_shape=(pltpu.VMEM((slots, blocks * kept, sample_...  1.95 us
    pallas_call x1, Pallas kernels, correlate(): pl.pallas_call(body, out_shape=jax.ShapeDtypeStruct(shape, jnp.float32),...  1.86 us
    ppermute x1, waiting for transfers between devices, local(): lax.ppermute(got, 'chan', [(group, group - 1) for group in range(1, group...  1.73 us
    ppermute x1, starting transfers between devices, local(): lax.ppermute(got, 'chan', [(group, group - 1) for group in range(1, group...  1.28 us
    pallas_call x1, Pallas kernels, prepare(): pl.pallas_call(body, out_shape=out_shape, in_specs=[pl.BlockSpec(memory_s...  1.26 us
  transfers between devices with their start and end apart: 1, of which 1 were waited for; matrix products, arithmetic and copies ran while one was open for 0% of the time, Pallas kernels for 5%

profile of v5, /device:TPU:0, one launch (start us, length us, event | category | flops | bytes accessed | tf_op | source)
XLA Modules:
  0.0 31.4 jit_solution(11519160640143330850)
XLA Ops:
  0.0 1.9 %normalize.1 = (bf16[4,64,512]{2,1,0:T(8,128)(2,1)S(1)}, s32[8,128]{1,0:T(8,128)S(1)}) custom-call(f32[16,4,16,128]{3,2,1,0:T(8,128)} %bitcast.10, f32[1,128]{1,0:T(1,128)} %bitcast.13, s32[1,256]{1,0:T(1,128)} %bitcast.11, s32[1,256]{1,0:T(1,128)} %bitcast.12, s32[1,4]{1,0:T(1,128)} %bitcast.14, s32[1,4]{1,0:T(1,128)} %bitcast.15), custom_call_target="tpu_custom_call" | custom-call | tf_op jit(solution)/shard_map/normalize/pallas_call | solution.py:119
  2.0 17.8 %all_to_all.5.refs_1_.refs_2_ = bf16[32,8,512]{2,1,0:T(8,128)(2,1)S(1)} all-to-all(bf16[32,8,512]{2,1,0:T(8,128)(2,1)S(1)} %bitcast.8), channel_id=1, replica_groups=mesh['tm'=4,'chan'=8] {'tm','chan'}, dimensions={0} | all-to-all | bytes 524288 | tf_op jit(solution)/shard_map/all_to_all | solution.py:354
  19.7 1.3 %collective-permute-start = (bf16[32,8,512]{2,1,0:T(8,128)(2,1)S(1)}, bf16[32,8,512]{2,1,0:T(8,128)(2,1)S(1)}, u32[]{:S(2)}, u32[]{:S(2)}) collective-permute-start(bf16[32,8,512]{2,1,0:T(8,128)(2,1)S(1)} %all_to_all.5.refs_1_.refs_2_), channel_id=1, source_target_pairs={{1,0},{2,1},{3,2},{4,3},{5,4},{6,5},{7,6},{9,8},{10,9},{11,10},{12... | collective-permute-start | bytes 786440 | tf_op jit(solution)/shard_map/ppermute | solution.py:361
  21.0 0.3 %pick_sources.1 = bf16[16,512]{1,0:T(8,128)(2,1)S(1)} custom-call(s32[8,128]{1,0:T(8,128)S(1)} %get-tuple-element.9.refs_0_, bf16[32,8,512]{2,1,0:T(8,128)(2,1)S(1)} %all_to_all.5.refs_1_.refs_2_), custom_call_target="tpu_custom_call" | custom-call | tf_op jit(solution)/shard_map/pick_sources/pallas_call | solution.py:170
  21.3 5.2 %all-gather = bf16[64,512]{1,0:T(8,128)(2,1)S(1)} all-gather(bf16[16,512]{1,0:T(8,128)(2,1)S(1)} %pick_sources.1), channel_id=2, replica_groups=mesh['tm'=4,'chan'=8] {'tm'}, dimensions={0}, use_global_device_ids=true | all-gather | bytes 81920 | tf_op jit(solution)/shard_map/all_gather | solution.py:363
  26.6 1.3 %prepare.1 = (bf16[16,128,640]{2,1,0:T(8,128)(2,1)S(1)}, bf16[2,4,32,512]{3,2,1,0:T(8,128)(2,1)S(1)}) custom-call(s32[8,128]{1,0:T(8,128)S(1)} %get-tuple-element.9.refs_0_, bf16[4,16,512]{2,1,0:T(8,128)(2,1)S(1)} %bitcast.9, bf16[32,8,512]{2,1,0:T(8,128)(2,1)S(1)} %all_to_all.5.refs_1_.refs_2_), custom_call_target="tpu_custom_call" | custom-call | tf_op jit(solution)/shard_map/prepare/pallas_call | solution.py:225
  27.8 1.7 %collective-permute-done.refs_3_ = bf16[32,8,512]{2,1,0:T(8,128)(2,1)S(1)} collective-permute-done((bf16[32,8,512]{2,1,0:T(8,128)(2,1)S(1)}, bf16[32,8,512]{2,1,0:T(8,128)(2,1)S(1)}, u32[]{:S(2)}, u32[]{:S(2)}) %collective-permute-start) | collective-permute-done | bytes 262176 | tf_op jit(solution)/shard_map/ppermute | solution.py:361
  29.6 1.9 %correlate.1 = f32[32,4,1024]{2,1,0:T(4,128)} custom-call(s32[8,128]{1,0:T(8,128)S(1)} %get-tuple-element.9.refs_0_, bf16[16,128,640]{2,1,0:T(8,128)(2,1)S(1)} %get-tuple-element.11.refs_1_, bf16[2,4,32,512]{3,2,1,0:T(8,128)(2,1)S(1)} %get-tuple-element.12.refs_2_, bf16[32,8,512]{2,1,0:T(8,128)(2,1)S(1)} %collective-permute-done.refs_3_), custom_call_target="tpu_custom_call" | custom-call | tf_op jit(solution)/shard_map/correlate/pallas_call | solution.py:325
Async XLA Ops:
  19.7 9.8 %collective-permute-start = (bf16[32,8,512]{2,1,0:T(8,128)(2,1)S(1)}, bf16[32,8,512]{2,1,0:T(8,128)(2,1)S(1)}, u32[]{:S(2)}, u32[]{:S(2)}) collective-permute-start(bf16[32,8,512]{2,1,0:T(8,128)(2,1)S(1)} %all_to_all.5.refs_1_.refs_2_), channel_id=1, source_target_pairs={{1,0},{2,1},{3,2},{4,3},{5,4},{6,5},{7,6},{9,8},{10,9},{11,10},{12... | collective-permute-start | bytes 786440 | tf_op jit(solution)/shard_map/ppermute | solution.py:361

commit v6 on v5

--- a/solution.py
+++ b/solution.py
@@ -179,26 +179,31 @@
     )(near_core(index), near_core(got))
 
 
-def merge_in_kernel(got_ref, merged_ref, units):
-    upper = lax.broadcasted_iota(jnp.int32, (8, merged_ref.shape[3]), 0) < 4
+def merge_in_kernel(got_ref, merged_ref, spread_ref, units):
+    sample_count = merged_ref.shape[3]
     for segment in range(merged_ref.shape[1]):
-        for first in range(0, units, 4):
-            parts = [[], []]
-            for unit in (first, first + 2):
-                a = got_ref[segment * units + unit].astype(jnp.float32)
-                b = got_ref[segment * units + unit + 1].astype(jnp.float32)
-                parts[0].append(jnp.where(upper, a, pltpu.roll(b, 4, 0)))
-                parts[1].append(jnp.where(upper, pltpu.roll(a, 4, 0), b))
+        for chunk in range(sample_count // LANES):
+            low = chunk * LANES
+            tile = got_ref[segment * units : (segment + 1) * units, :, low : low + LANES]
+            spread_ref[segment, chunk] = tile.astype(jnp.float32).reshape(units * 8, LANES)
             for block in range(2):
-                merged_ref[block, segment, first * 4 : first * 4 + 16, :] = jnp.concatenate(
-                    parts[block], axis=0
+                rows = [
+                    spread_ref[segment, chunk, pl.ds(block * 4 + place, units, stride=8), :]
+                    for place in range(4)
+                ]
+                merged_ref[block, segment, :, low : low + LANES] = jnp.concatenate(
+                    rows, axis=0
                 ).astype(jnp.bfloat16)
+
+
+def spread_like(segments, sample_count, units):
+    return pltpu.VMEM((segments, sample_count // LANES, units * 8, LANES), jnp.float32)
 
 
 def prepare_kernel(owned, units, merged_here, index_ref, source_ref, *refs):
     if merged_here:
-        own_ref, moved_ref, merged_ref = refs
-        merge_in_kernel(own_ref, merged_ref, units)
+        own_ref, moved_ref, merged_ref, spread_ref = refs
+        merge_in_kernel(own_ref, merged_ref, spread_ref, units)
     else:
         (moved_ref,) = refs
     segments = source_ref.shape[1] // PAIR_DEV
@@ -214,10 +219,13 @@
 
 def prepare(index, sources, own, owned, units):
     count, sample_count = sources.shape[1:]
+    segments = count // PAIR_DEV
     out_shape = [pltpu.VMEM((count, LANES, sample_count + LANES), jnp.bfloat16)]
+    scratch = []
     if own:
-        merged = (NEAR // 2, count // PAIR_DEV, owned, sample_count)
+        merged = (NEAR // 2, segments, owned, sample_count)
         out_shape.append(pltpu.VMEM(merged, jnp.bfloat16))
+        scratch.append(spread_like(segments, sample_count, units))
 
     def body(*refs):
         prepare_kernel(owned, units, bool(own), *refs)
@@ -227,6 +235,7 @@
         out_shape=out_shape,
         in_specs=[pl.BlockSpec(memory_space=pltpu.VMEM)] * (2 + len(own)),
         out_specs=[pl.BlockSpec(memory_space=pltpu.VMEM)] * len(out_shape),
+        scratch_shapes=scratch,
         compiler_params=pltpu.CompilerParams(vmem_limit_bytes=KERNEL_VMEM),
         name="prepare",
     )(near_core(index), near_core(sources), *map(near_core, own))
@@ -272,19 +281,19 @@
     return sums
 
 
-def correlate_kernel(owned, kept, units, merged_here, index_ref, moved_ref, *refs):
+def correlate_kernel(units, merged_here, index_ref, moved_ref, *refs):
     if merged_here:
-        own_ref, next_ref, out_hbm, lines_ref, out_ref, sems, after_ref = refs
-        merge_in_kernel(next_ref, after_ref, units)
+        own_ref, next_ref, out_hbm, out_ref, sems, after_ref, spread_ref = refs
         segments, _, sample_count = own_ref.shape[1:]
     else:
-        merged_ref, out_hbm, lines_ref, out_ref, sems = refs
+        merged_ref, out_hbm, out_ref, sems = refs
         segments, _, sample_count = merged_ref.shape[1:]
     factor = 1.0 / math.sqrt(sample_count * segments)
-    across = owned // kept
+    picked = [index_at(index_ref, PAIR_DEV + pair) for pair in range(PAIR_DEV)]
+    if merged_here:
+        merge_in_kernel(next_ref, after_ref, spread_ref, units)
     copies = []
-    for pair in range(PAIR_DEV):
-        block = index_at(index_ref, PAIR_DEV + pair)
+    for pair, block in enumerate(picked):
         if merged_here:
             ahead = block >= NEAR // 2
             place = block % (NEAR // 2)
@@ -295,12 +304,7 @@
             receivers = [merged_ref[block, i] for i in range(segments)]
         sums = lag_products(receivers, [moved_ref[pair * segments + i] for i in range(segments)])
         for chunk, part in enumerate(sums):
-            lines_ref[chunk] = part * factor
-            low = chunk * LANES
-            for place in range(kept):
-                out_ref[place * across : (place + 1) * across, pair, low : low + LANES] = (
-                    lines_ref[chunk, pl.ds(place, across, stride=kept), :]
-                )
+            out_ref[:, pair, chunk * LANES : (chunk + 1) * LANES] = part * factor
         copy = pltpu.make_async_copy(out_ref.at[:, pair], out_hbm.at[:, pair], sems.at[pair])
         copy.start()
         copies.append(copy)
@@ -308,20 +312,21 @@
         copy.wait()
 
 
-def correlate(index, toeplitz, receivers, owned, kept, units):
+def correlate(index, toeplitz, receivers, owned, units):
     merged_here = len(receivers) == 2
     shape = (owned, PAIR_DEV, 2 * MAX_LAG)
 
     def body(*refs):
-        correlate_kernel(owned, kept, units, merged_here, *refs)
+        correlate_kernel(units, merged_here, *refs)
 
     scratch = [
-        pltpu.VMEM((2 * MAX_LAG // LANES, owned, LANES), jnp.float32),
         pltpu.VMEM(shape, jnp.float32),
         pltpu.SemaphoreType.DMA((PAIR_DEV,)),
     ]
     if merged_here:
-        scratch.append(pltpu.VMEM(receivers[0].shape, jnp.bfloat16))
+        own = receivers[0]
+        scratch.append(pltpu.VMEM(own.shape, own.dtype))
+        scratch.append(spread_like(own.shape[1], own.shape[3], units))
     return pl.pallas_call(
         body,
         out_shape=jax.ShapeDtypeStruct(shape, jnp.float32),
@@ -363,14 +368,14 @@
     sources = lax.all_gather(picked, "tm")
     if kept == 4 and owned == 4 * units and near == 2:
         toeplitz, own = prepare(index, sources, (got,), owned, units)
-        return correlate(index, toeplitz, (own, following), owned, kept, units)
+        return correlate(index, toeplitz, (own, following), owned, units)
     across = owned // kept
     first = lax.axis_index("tm") * owned % units
     apart = [x.reshape(segments, units, near, kept, sample_count) for x in (got, following)]
     apart = lax.dynamic_slice_in_dim(jnp.concatenate(apart, axis=2), first, across, axis=1)
-    merged = apart.transpose(2, 0, 1, 3, 4).reshape(2 * near, segments, owned, sample_count)
+    merged = apart.transpose(2, 0, 3, 1, 4).reshape(2 * near, segments, owned, sample_count)
     (toeplitz,) = prepare(index, sources, (), owned, units)
-    return correlate(index, toeplitz, (merged,), owned, kept, units)
+    return correlate(index, toeplitz, (merged,), owned, units)
 
 
 def solution(mesh):

time: 31.6 us -> 31.4 us (level)
  no operation moved by 1% of the time
where the time goes in v6:
time: 31.4 us; the launch traced here: 31.2 us
  blocking collectives  23 us (73%)
  Pallas kernels  5.23 us (17%)
  waiting for transfers between devices  1.72 us (5%)
  starting transfers between devices  1.28 us (4%)
    all_to_all x1, blocking collectives, local(): lax.all_to_all(sent.reshape(segments * groups, near * kept, sample_count)...  17.8 us
    all_gather x1, blocking collectives, local(): sources = lax.all_gather(picked, 'tm')  5.23 us
    pallas_call x1, Pallas kernels, normalize(): pl.pallas_call(body, out_shape=(pltpu.VMEM((slots, blocks * kept, sample_...  1.95 us
    ppermute x1, waiting for transfers between devices, local(): lax.ppermute(got, 'chan', [(group, group - 1) for group in range(1, group...  1.72 us
    pallas_call x1, Pallas kernels, correlate(): pl.pallas_call(body, out_shape=jax.ShapeDtypeStruct(shape, jnp.float32),...  1.69 us
    ppermute x1, starting transfers between devices, local(): lax.ppermute(got, 'chan', [(group, group - 1) for group in range(1, group...  1.28 us
    pallas_call x1, Pallas kernels, prepare(): pl.pallas_call(body, out_shape=out_shape, in_specs=[pl.BlockSpec(memory_s...  1.26 us
  transfers between devices with their start and end apart: 1, of which 1 were waited for; matrix products, arithmetic and copies ran while one was open for 0% of the time, Pallas kernels for 5%

profile of v6, /device:TPU:0, one launch (start us, length us, event | category | flops | bytes accessed | tf_op | source)
XLA Modules:
  0.0 31.2 jit_solution(9517898341929259642)
XLA Ops:
  0.0 1.9 %normalize.1 = (bf16[4,64,512]{2,1,0:T(8,128)(2,1)S(1)}, s32[8,128]{1,0:T(8,128)S(1)}) custom-call(f32[16,4,16,128]{3,2,1,0:T(8,128)} %bitcast.10, f32[1,128]{1,0:T(1,128)} %bitcast.13, s32[1,256]{1,0:T(1,128)} %bitcast.11, s32[1,256]{1,0:T(1,128)} %bitcast.12, s32[1,4]{1,0:T(1,128)} %bitcast.14, s32[1,4]{1,0:T(1,128)} %bitcast.15), custom_call_target="tpu_custom_call" | custom-call | tf_op jit(solution)/shard_map/normalize/pallas_call | solution.py:119
  2.0 17.8 %all_to_all.5.refs_1_.refs_2_ = bf16[32,8,512]{2,1,0:T(8,128)(2,1)S(1)} all-to-all(bf16[32,8,512]{2,1,0:T(8,128)(2,1)S(1)} %bitcast.8), channel_id=1, replica_groups=mesh['tm'=4,'chan'=8] {'tm','chan'}, dimensions={0} | all-to-all | bytes 524288 | tf_op jit(solution)/shard_map/all_to_all | solution.py:359
  19.7 1.3 %collective-permute-start = (bf16[32,8,512]{2,1,0:T(8,128)(2,1)S(1)}, bf16[32,8,512]{2,1,0:T(8,128)(2,1)S(1)}, u32[]{:S(2)}, u32[]{:S(2)}) collective-permute-start(bf16[32,8,512]{2,1,0:T(8,128)(2,1)S(1)} %all_to_all.5.refs_1_.refs_2_), channel_id=1, source_target_pairs={{1,0},{2,1},{3,2},{4,3},{5,4},{6,5},{7,6},{9,8},{10,9},{11,10},{12... | collective-permute-start | bytes 786440 | tf_op jit(solution)/shard_map/ppermute | solution.py:366
  21.0 0.3 %pick_sources.1 = bf16[16,512]{1,0:T(8,128)(2,1)S(1)} custom-call(s32[8,128]{1,0:T(8,128)S(1)} %get-tuple-element.9.refs_0_, bf16[32,8,512]{2,1,0:T(8,128)(2,1)S(1)} %all_to_all.5.refs_1_.refs_2_), custom_call_target="tpu_custom_call" | custom-call | tf_op jit(solution)/shard_map/pick_sources/pallas_call | solution.py:170
  21.3 5.2 %all-gather = bf16[64,512]{1,0:T(8,128)(2,1)S(1)} all-gather(bf16[16,512]{1,0:T(8,128)(2,1)S(1)} %pick_sources.1), channel_id=2, replica_groups=mesh['tm'=4,'chan'=8] {'tm'}, dimensions={0}, use_global_device_ids=true | all-gather | bytes 81920 | tf_op jit(solution)/shard_map/all_gather | solution.py:368
  26.6 1.3 %prepare.1 = (bf16[16,128,640]{2,1,0:T(8,128)(2,1)S(1)}, bf16[2,4,32,512]{3,2,1,0:T(8,128)(2,1)S(1)}) custom-call(s32[8,128]{1,0:T(8,128)S(1)} %get-tuple-element.9.refs_0_, bf16[4,16,512]{2,1,0:T(8,128)(2,1)S(1)} %bitcast.9, bf16[32,8,512]{2,1,0:T(8,128)(2,1)S(1)} %all_to_all.5.refs_1_.refs_2_), custom_call_target="tpu_custom_call" | custom-call | tf_op jit(solution)/shard_map/prepare/pallas_call | solution.py:233
  27.8 1.7 %collective-permute-done.refs_3_ = bf16[32,8,512]{2,1,0:T(8,128)(2,1)S(1)} collective-permute-done((bf16[32,8,512]{2,1,0:T(8,128)(2,1)S(1)}, bf16[32,8,512]{2,1,0:T(8,128)(2,1)S(1)}, u32[]{:S(2)}, u32[]{:S(2)}) %collective-permute-start) | collective-permute-done | bytes 262176 | tf_op jit(solution)/shard_map/ppermute | solution.py:366
  29.6 1.7 %correlate.1 = f32[32,4,1024]{2,1,0:T(4,128)} custom-call(s32[8,128]{1,0:T(8,128)S(1)} %get-tuple-element.9.refs_0_, bf16[16,128,640]{2,1,0:T(8,128)(2,1)S(1)} %get-tuple-element.11.refs_1_, bf16[2,4,32,512]{3,2,1,0:T(8,128)(2,1)S(1)} %get-tuple-element.12.refs_2_, bf16[32,8,512]{2,1,0:T(8,128)(2,1)S(1)} %collective-permute-done.refs_3_), custom_call_target="tpu_custom_call" | custom-call | tf_op jit(solution)/shard_map/correlate/pallas_call | solution.py:330
Async XLA Ops:
  19.7 9.8 %collective-permute-start = (bf16[32,8,512]{2,1,0:T(8,128)(2,1)S(1)}, bf16[32,8,512]{2,1,0:T(8,128)(2,1)S(1)}, u32[]{:S(2)}, u32[]{:S(2)}) collective-permute-start(bf16[32,8,512]{2,1,0:T(8,128)(2,1)S(1)} %all_to_all.5.refs_1_.refs_2_), channel_id=1, source_target_pairs={{1,0},{2,1},{3,2},{4,3},{5,4},{6,5},{7,6},{9,8},{10,9},{11,10},{12... | collective-permute-start | bytes 786440 | tf_op jit(solution)/shard_map/ppermute | solution.py:366

commit v7 on v6

--- a/solution.py
+++ b/solution.py
@@ -19,6 +19,10 @@
     return pltpu.with_memory_space_constraint(x, pltpu.VMEM)
 
 
+def in_scalar(x):
+    return pltpu.with_memory_space_constraint(x, pltpu.SMEM)
+
+
 def toeplitz_rows(row, width, first=0):
     return pltpu.roll(
         jnp.broadcast_to(row, (LANES, width)), first, 1, stride=1, stride_axis=0
@@ -33,12 +37,9 @@
 
 
 def normalize_kernel(slots, kept, rec_hbm, *refs):
-    small_refs, (out_ref, index_ref, rec_ref), small_bufs, sems = (
-        refs[:5],
-        refs[5:8],
-        refs[8:13],
-        refs[13],
-    )
+    small_refs, out_ref = refs[:5], refs[5]
+    rec_ref, taps_ref, start_ref, extent_ref, sems = refs[8:]
+    small_bufs = (taps_ref, start_ref, extent_ref, refs[6], refs[7])
     blocks = rec_hbm.shape[0]
     rows = blocks * kept
     pieces = rec_hbm.shape[2] // kept
@@ -55,16 +56,11 @@
         copies.append(copy)
     for copy in small:
         copy.wait()
-    taps_ref, start_ref, extent_ref, channel_ref, block_ref = small_bufs
     taps = jnp.concatenate([taps_ref[...], jnp.zeros((1, LANES), jnp.float32)], axis=1)
     w0, w1, w2 = in_parts(toeplitz_rows(taps, 2 * LANES))
     weights = jnp.concatenate([w0, w0, w0, w1, w1, w2], axis=0)
     starts = start_ref[...].astype(jnp.float32)
     ends = starts + extent_ref[...].astype(jnp.float32)
-    for i, ref in enumerate((channel_ref, block_ref)):
-        for pair in range(PAIR_DEV):
-            value = jnp.broadcast_to(ref[:, pair : pair + 1], (1, LANES))
-            index_ref[i * PAIR_DEV + pair : i * PAIR_DEV + pair + 1, :] = value
     round_count = starts.shape[1]
     lane = lax.broadcasted_iota(jnp.int32, (rows, round_count), 1)
     row = lax.broadcasted_iota(jnp.int32, (rows, round_count), 0)
@@ -120,30 +116,28 @@
         body,
         out_shape=(
             pltpu.VMEM((slots, blocks * kept, sample_count), jnp.bfloat16),
-            pltpu.VMEM((2 * PAIR_DEV, LANES), jnp.int32),
+            pltpu.SMEM((PAIR_DEV,), jnp.int32),
+            pltpu.SMEM((PAIR_DEV,), jnp.int32),
         ),
         in_specs=[pl.BlockSpec(memory_space=pl.ANY)] * (1 + len(small)),
-        out_specs=[pl.BlockSpec(memory_space=pltpu.VMEM)] * 2,
+        out_specs=[pl.BlockSpec(memory_space=pltpu.VMEM)]
+        + [pl.BlockSpec(memory_space=pltpu.SMEM)] * 2,
         scratch_shapes=[
             pltpu.VMEM((slots, blocks, kept * pieces, LANES), jnp.float32),
-            *[pltpu.VMEM(x.shape, x.dtype) for x in small],
+            *[pltpu.VMEM(x.shape, x.dtype) for x in small[:3]],
             pltpu.SemaphoreType.DMA((slots + len(small),)),
         ],
         name="normalize",
     )(view, *small)
 
 
-def index_at(index_ref, row):
-    return jnp.max(index_ref[row : row + 1, :].astype(jnp.float32)).astype(jnp.int32)
-
-
-def pick_kernel(units, kept, segments, index_ref, got_ref, out_ref):
+def pick_kernel(units, kept, segments, channel_ref, got_ref, out_ref):
     sample_count = got_ref.shape[2]
     shape = got_ref.shape[1:]
     row = lax.broadcasted_iota(jnp.int32, shape, 0)
     found = []
     for pair in range(PAIR_DEV):
-        channel = index_at(index_ref, pair)
+        channel = channel_ref[pair]
         unit = channel % units
         wanted = row == (channel // BLOCK) * kept + ((channel % BLOCK) // units) % kept
         for segment in range(segments):
@@ -161,7 +155,7 @@
         ).astype(out_ref.dtype)
 
 
-def pick_sources(index, got, units, kept, segments):
+def pick_sources(channels, got, units, kept, segments):
     count = PAIR_DEV * segments
 
     def body(*refs):
@@ -171,12 +165,12 @@
         body,
         out_shape=pltpu.VMEM((count, got.shape[2]), jnp.bfloat16),
         in_specs=[
-            pl.BlockSpec(memory_space=pltpu.VMEM),
+            pl.BlockSpec(memory_space=pltpu.SMEM),
             pl.BlockSpec(memory_space=pltpu.VMEM),
         ],
         out_specs=pl.BlockSpec(memory_space=pltpu.VMEM),
         name="pick_sources",
-    )(near_core(index), near_core(got))
+    )(in_scalar(channels), near_core(got))
 
 
 def merge_in_kernel(got_ref, merged_ref, spread_ref, units):
@@ -200,7 +194,7 @@
     return pltpu.VMEM((segments, sample_count // LANES, units * 8, LANES), jnp.float32)
 
 
-def prepare_kernel(owned, units, merged_here, index_ref, source_ref, *refs):
+def prepare_kernel(owned, units, merged_here, channel_ref, source_ref, *refs):
     if merged_here:
         own_ref, moved_ref, merged_ref, spread_ref = refs
         merge_in_kernel(own_ref, merged_ref, spread_ref, units)
@@ -209,7 +203,7 @@
     segments = source_ref.shape[1] // PAIR_DEV
     spare = jnp.zeros((1, LANES), jnp.float32)
     for pair in range(PAIR_DEV):
-        holder = (index_at(index_ref, pair) % BLOCK) // owned
+        holder = (channel_ref[pair] % BLOCK) // owned
         for segment in range(segments):
             at = pair * segments + segment
             line = source_ref[holder, at : at + 1, :].astype(jnp.float32)
@@ -217,7 +211,7 @@
             moved_ref[at] = toeplitz_rows(line, line.shape[1], 1).astype(jnp.bfloat16)
 
 
-def prepare(index, sources, own, owned, units):
+def prepare(channels, sources, own, owned, units):
     count, sample_count = sources.shape[1:]
     segments = count // PAIR_DEV
     out_shape = [pltpu.VMEM((count, LANES, sample_count + LANES), jnp.bfloat16)]
@@ -233,12 +227,13 @@
     return pl.pallas_call(
         body,
         out_shape=out_shape,
-        in_specs=[pl.BlockSpec(memory_space=pltpu.VMEM)] * (2 + len(own)),
+        in_specs=[pl.BlockSpec(memory_space=pltpu.SMEM)]
+        + [pl.BlockSpec(memory_space=pltpu.VMEM)] * (1 + len(own)),
         out_specs=[pl.BlockSpec(memory_space=pltpu.VMEM)] * len(out_shape),
         scratch_shapes=scratch,
         compiler_params=pltpu.CompilerParams(vmem_limit_bytes=KERNEL_VMEM),
         name="prepare",
-    )(near_core(index), near_core(sources), *map(near_core, own))
+    )(in_scalar(channels), near_core(sources), *map(near_core, own))
 
 
 def lag_products(receivers, toeplitz):
@@ -281,7 +276,7 @@
     return sums
 
 
-def correlate_kernel(units, merged_here, index_ref, moved_ref, *refs):
+def correlate_kernel(units, merged_here, block_ref, moved_ref, *refs):
     if merged_here:
         own_ref, next_ref, out_hbm, out_ref, sems, after_ref, spread_ref = refs
         segments, _, sample_count = own_ref.shape[1:]
@@ -289,11 +284,11 @@
         merged_ref, out_hbm, out_ref, sems = refs
         segments, _, sample_count = merged_ref.shape[1:]
     factor = 1.0 / math.sqrt(sample_count * segments)
-    picked = [index_at(index_ref, PAIR_DEV + pair) for pair in range(PAIR_DEV)]
     if merged_here:
         merge_in_kernel(next_ref, after_ref, spread_ref, units)
     copies = []
-    for pair, block in enumerate(picked):
+    for pair in range(PAIR_DEV):
+        block = block_ref[pair]
         if merged_here:
             ahead = block >= NEAR // 2
             place = block % (NEAR // 2)
@@ -312,7 +307,7 @@
         copy.wait()
 
 
-def correlate(index, toeplitz, receivers, owned, units):
+def correlate(chosen, toeplitz, receivers, owned, units):
     merged_here = len(receivers) == 2
     shape = (owned, PAIR_DEV, 2 * MAX_LAG)
 
@@ -330,12 +325,13 @@
     return pl.pallas_call(
         body,
         out_shape=jax.ShapeDtypeStruct(shape, jnp.float32),
-        in_specs=[pl.BlockSpec(memory_space=pltpu.VMEM)] * (2 + len(receivers)),
+        in_specs=[pl.BlockSpec(memory_space=pltpu.SMEM)]
+        + [pl.BlockSpec(memory_space=pltpu.VMEM)] * (1 + len(receivers)),
         out_specs=pl.BlockSpec(memory_space=pl.ANY),
         scratch_shapes=scratch,
         compiler_params=pltpu.CompilerParams(vmem_limit_bytes=KERNEL_VMEM),
         name="correlate",
-    )(near_core(index), near_core(toeplitz), *map(near_core, receivers))
+    )(in_scalar(chosen), near_core(toeplitz), *map(near_core, receivers))
 
 
 def local(recordings, gap_start, dropout_extent, filter_taps, source_channel, receiver_block):
@@ -349,11 +345,9 @@
     rounds_block = BLOCK // units
     slots = min(segments, rounds_block)
     kept = rounds_block // slots
-    small = [
-        x.reshape(1, x.size)
-        for x in (filter_taps, gap_start, dropout_extent, source_channel, receiver_block)
-    ]
-    normalized, index = normalize(recordings, small, blocks, slots, kept)
+    small = [x.reshape(1, x.size) for x in (filter_taps, gap_start, dropout_extent)]
+    small += [source_channel, receiver_block]
+    normalized, channels, chosen = normalize(recordings, small, blocks, slots, kept)
     sent = normalized.reshape(slots, groups, near * kept, sample_count)
     sent = jnp.repeat(sent, segments // slots, axis=0) if segments > slots else sent
     got = lax.all_to_all(
@@ -364,18 +358,18 @@
         tiled=True,
     )
     following = lax.ppermute(got, "chan", [(group, group - 1) for group in range(1, groups)])
-    picked = pick_sources(index, got, units, kept, segments)
+    picked = pick_sources(channels, got, units, kept, segments)
     sources = lax.all_gather(picked, "tm")
     if kept == 4 and owned == 4 * units and near == 2:
-        toeplitz, own = prepare(index, sources, (got,), owned, units)
-        return correlate(index, toeplitz, (own, following), owned, units)
+        toeplitz, own = prepare(channels, sources, (got,), owned, units)
+        return correlate(chosen, toeplitz, (own, following), owned, units)
     across = owned // kept
     first = lax.axis_index("tm") * owned % units
     apart = [x.reshape(segments, units, near, kept, sample_count) for x in (got, following)]
     apart = lax.dynamic_slice_in_dim(jnp.concatenate(apart, axis=2), first, across, axis=1)
     merged = apart.transpose(2, 0, 3, 1, 4).reshape(2 * near, segments, owned, sample_count)
-    (toeplitz,) = prepare(index, sources, (), owned, units)
-    return correlate(index, toeplitz, (merged,), owned, units)
+    (toeplitz,) = prepare(channels, sources, (), owned, units)
+    return correlate(chosen, toeplitz, (merged,), owned, units)
 
 
 def solution(mesh):

time: 31.4 us -> 31.4 us (level)
  Pallas kernels: 5.23 us -> 4.57 us
  waiting for transfers between devices: 1.72 us -> 2.33 us
    ppermute x1, waiting for transfers between devices: 1.72 us -> 2.33 us  [local(): lax.ppermute(got, 'chan', [(group, group - 1) for group in range(1, group...]
    pallas_call x1, Pallas kernels: 1.26 us -> 0.76 us  [prepare(): pl.pallas_call(body, out_shape=out_shape, in_specs=[pl.BlockSpec(memory_s...]
  transfers between devices with their start and end apart: 1 -> 1, of which waited for: 1 -> 1; matrix products, arithmetic and copies ran while one was open for 0% -> 0% of each run, Pallas kernels for 5% -> 3%
where the time goes in v7:
time: 31.4 us; the launch traced here: 31.2 us
  blocking collectives  23 us (73%)
  Pallas kernels  4.57 us (15%)
  waiting for transfers between devices  2.33 us (7%)
  starting transfers between devices  1.28 us (4%)
    all_to_all x1, blocking collectives, local(): lax.all_to_all(sent.reshape(segments * groups, near * kept, sample_count)...  17.8 us
    all_gather x1, blocking collectives, local(): sources = lax.all_gather(picked, 'tm')  5.23 us
    ppermute x1, waiting for transfers between devices, local(): lax.ppermute(got, 'chan', [(group, group - 1) for group in range(1, group...  2.33 us
    pallas_call x1, Pallas kernels, normalize(): pl.pallas_call(body, out_shape=(pltpu.VMEM((slots, blocks * kept, sample_...  1.91 us
    pallas_call x1, Pallas kernels, correlate(): pl.pallas_call(body, out_shape=jax.ShapeDtypeStruct(shape, jnp.float32),...  1.67 us
    ppermute x1, starting transfers between devices, local(): lax.ppermute(got, 'chan', [(group, group - 1) for group in range(1, group...  1.28 us
    pallas_call x1, Pallas kernels, prepare(): pl.pallas_call(body, out_shape=out_shape, in_specs=[pl.BlockSpec(memory_s...  0.76 us
  transfers between devices with their start and end apart: 1, of which 1 were waited for; matrix products, arithmetic and copies ran while one was open for 0% of the time, Pallas kernels for 3%

profile of v7, /device:TPU:0, one launch (start us, length us, event | category | flops | bytes accessed | tf_op | source)
XLA Modules:
  0.0 31.2 jit_solution(14209393401233550912)
XLA Ops:
  0.0 1.9 %normalize.1 = (bf16[4,64,512]{2,1,0:T(8,128)(2,1)S(1)}, s32[4]{0:T(128)S(4)}, s32[4]{0:T(128)S(4)}) custom-call(f32[16,4,16,128]{3,2,1,0:T(8,128)} %bitcast.8, f32[1,128]{1,0:T(1,128)} %bitcast.11, s32[1,256]{1,0:T(1,128)} %bitcast.9, s32[1,256]{1,0:T(1,128)} %bitcast.10, s32[4]{0:T(128)} %refs_4_.1, s32[4]{0:T(128)} %refs_5_.1), custom_call_target="tpu_custom_call" | custom-call | tf_op jit(solution)/shard_map/normalize/pallas_call | solution.py:115
  1.9 17.8 %all_to_all.5.refs_1_.refs_2_ = bf16[32,8,512]{2,1,0:T(8,128)(2,1)S(1)} all-to-all(bf16[32,8,512]{2,1,0:T(8,128)(2,1)S(1)} %bitcast.7), channel_id=1, replica_groups=mesh['tm'=4,'chan'=8] {'tm','chan'}, dimensions={0} | all-to-all | bytes 524288 | tf_op jit(solution)/shard_map/all_to_all | solution.py:353
  19.7 1.3 %collective-permute-start = (bf16[32,8,512]{2,1,0:T(8,128)(2,1)S(1)}, bf16[32,8,512]{2,1,0:T(8,128)(2,1)S(1)}, u32[]{:S(2)}, u32[]{:S(2)}) collective-permute-start(bf16[32,8,512]{2,1,0:T(8,128)(2,1)S(1)} %all_to_all.5.refs_1_.refs_2_), channel_id=1, source_target_pairs={{1,0},{2,1},{3,2},{4,3},{5,4},{6,5},{7,6},{9,8},{10,9},{11,10},{12... | collective-permute-start | bytes 786440 | tf_op jit(solution)/shard_map/ppermute | solution.py:360
  21.0 0.2 pick_sources.1
  21.2 5.2 %all-gather = bf16[64,512]{1,0:T(8,128)(2,1)S(1)} all-gather(bf16[16,512]{1,0:T(8,128)(2,1)S(1)} %pick_sources.1), channel_id=2, replica_groups=mesh['tm'=4,'chan'=8] {'tm'}, dimensions={0}, use_global_device_ids=true | all-gather | bytes 81920 | tf_op jit(solution)/shard_map/all_gather | solution.py:362
  26.4 0.8 %prepare.1 = (bf16[16,128,640]{2,1,0:T(8,128)(2,1)S(1)}, bf16[2,4,32,512]{3,2,1,0:T(8,128)(2,1)S(1)}) custom-call(s32[4]{0:T(128)S(4)} %get-tuple-element.11.refs_0_, bf16[4,16,512]{2,1,0:T(8,128)(2,1)S(1)} %bitcast.6, bf16[32,8,512]{2,1,0:T(8,128)(2,1)S(1)} %all_to_all.5.refs_1_.refs_2_), custom_call_target="tpu_custom_call" | custom-call | tf_op jit(solution)/shard_map/prepare/pallas_call | solution.py:227
  27.2 2.3 %collective-permute-done.refs_3_ = bf16[32,8,512]{2,1,0:T(8,128)(2,1)S(1)} collective-permute-done((bf16[32,8,512]{2,1,0:T(8,128)(2,1)S(1)}, bf16[32,8,512]{2,1,0:T(8,128)(2,1)S(1)}, u32[]{:S(2)}, u32[]{:S(2)}) %collective-permute-start) | collective-permute-done | bytes 262176 | tf_op jit(solution)/shard_map/ppermute | solution.py:360
  29.5 1.7 %correlate.1 = f32[32,4,1024]{2,1,0:T(4,128)} custom-call(s32[4]{0:T(128)S(4)} %get-tuple-element.10.refs_0_, bf16[16,128,640]{2,1,0:T(8,128)(2,1)S(1)} %get-tuple-element.13.refs_1_, bf16[2,4,32,512]{3,2,1,0:T(8,128)(2,1)S(1)} %get-tuple-element.14.refs_2_, bf16[32,8,512]{2,1,0:T(8,128)(2,1)S(1)} %collective-permute-done.refs_3_), custom_call_target="tpu_custom_call" | custom-call | tf_op jit(solution)/shard_map/correlate/pallas_call | solution.py:325
Async XLA Ops:
  19.7 9.8 %collective-permute-start = (bf16[32,8,512]{2,1,0:T(8,128)(2,1)S(1)}, bf16[32,8,512]{2,1,0:T(8,128)(2,1)S(1)}, u32[]{:S(2)}, u32[]{:S(2)}) collective-permute-start(bf16[32,8,512]{2,1,0:T(8,128)(2,1)S(1)} %all_to_all.5.refs_1_.refs_2_), channel_id=1, source_target_pairs={{1,0},{2,1},{3,2},{4,3},{5,4},{6,5},{7,6},{9,8},{10,9},{11,10},{12... | collective-permute-start | bytes 786440 | tf_op jit(solution)/shard_map/ppermute | solution.py:360

commit v8 on v7

--- a/solution.py
+++ b/solution.py
@@ -276,30 +276,20 @@
     return sums
 
 
-def correlate_kernel(units, merged_here, block_ref, moved_ref, *refs):
-    if merged_here:
-        own_ref, next_ref, out_hbm, out_ref, sems, after_ref, spread_ref = refs
-        segments, _, sample_count = own_ref.shape[1:]
-    else:
-        merged_ref, out_hbm, out_ref, sems = refs
-        segments, _, sample_count = merged_ref.shape[1:]
+def store_sums(out_ref, slot, sums, factor):
+    for chunk, part in enumerate(sums):
+        out_ref[:, slot, chunk * LANES : (chunk + 1) * LANES] = part * factor
+
+
+def correlate_kernel(block_ref, moved_ref, merged_ref, out_hbm, out_ref, sems):
+    blocks, segments, _, sample_count = merged_ref.shape
     factor = 1.0 / math.sqrt(sample_count * segments)
-    if merged_here:
-        merge_in_kernel(next_ref, after_ref, spread_ref, units)
     copies = []
     for pair in range(PAIR_DEV):
-        block = block_ref[pair]
-        if merged_here:
-            ahead = block >= NEAR // 2
-            place = block % (NEAR // 2)
-            receivers = [
-                jnp.where(ahead, after_ref[place, i], own_ref[place, i]) for i in range(segments)
-            ]
-        else:
-            receivers = [merged_ref[block, i] for i in range(segments)]
+        place = block_ref[pair] % blocks
+        receivers = [merged_ref[place, i] for i in range(segments)]
         sums = lag_products(receivers, [moved_ref[pair * segments + i] for i in range(segments)])
-        for chunk, part in enumerate(sums):
-            out_ref[:, pair, chunk * LANES : (chunk + 1) * LANES] = part * factor
+        store_sums(out_ref, pair, sums, factor)
         copy = pltpu.make_async_copy(out_ref.at[:, pair], out_hbm.at[:, pair], sems.at[pair])
         copy.start()
         copies.append(copy)
@@ -307,31 +297,94 @@
         copy.wait()
 
 
-def correlate(chosen, toeplitz, receivers, owned, units):
-    merged_here = len(receivers) == 2
-    shape = (owned, PAIR_DEV, 2 * MAX_LAG)
+def correlate(chosen, toeplitz, merged):
+    shape = (merged.shape[2], PAIR_DEV, 2 * MAX_LAG)
+    return pl.pallas_call(
+        correlate_kernel,
+        out_shape=jax.ShapeDtypeStruct(shape, jnp.float32),
+        in_specs=[
+            pl.BlockSpec(memory_space=pltpu.SMEM),
+            pl.BlockSpec(memory_space=pltpu.VMEM),
+            pl.BlockSpec(memory_space=pltpu.VMEM),
+        ],
+        out_specs=pl.BlockSpec(memory_space=pl.ANY),
+        scratch_shapes=[
+            pltpu.VMEM(shape, jnp.float32),
+            pltpu.SemaphoreType.DMA((PAIR_DEV,)),
+        ],
+        compiler_params=pltpu.CompilerParams(vmem_limit_bytes=KERNEL_VMEM),
+        name="correlate",
+    )(in_scalar(chosen), near_core(toeplitz), near_core(merged))
+
+
+def ahead_kernel(
+    units, block_ref, moved_ref, next_ref, old_hbm, out_hbm, order_ref, after_ref, spread_ref, out_ref, sems
+):
+    blocks, segments, _, sample_count = after_ref.shape
+    factor = 1.0 / math.sqrt(sample_count * segments)
+    count = jnp.int32(0)
+    for pair in range(PAIR_DEV):
+        order_ref[count] = pair
+        count = count + jnp.where(block_ref[pair] >= blocks, 1, 0)
+
+    @pl.when(count > 0)
+    def _():
+        merge_in_kernel(next_ref, after_ref, spread_ref, units)
+
+    for first in range(0, PAIR_DEV, 2):
+
+        @pl.when(count > first)
+        def _(first=first):
+            for slot in (first, first + 1):
+                pair = order_ref[jnp.minimum(slot, count - 1)]
+                place = block_ref[pair] - blocks
+                receivers = [after_ref[place, i] for i in range(segments)]
+                moved = [moved_ref[pair * segments + i] for i in range(segments)]
+                store_sums(out_ref, slot, lag_products(receivers, moved), factor)
+
+            for slot in (first, first + 1):
+                for pair in range(PAIR_DEV):
+
+                    @pl.when((count > slot) & (order_ref[jnp.minimum(slot, count - 1)] == pair))
+                    def _(slot=slot, pair=pair):
+                        pltpu.make_async_copy(
+                            out_ref.at[:, slot], out_hbm.at[:, pair], sems.at[slot]
+                        ).start()
+
+    for slot in range(PAIR_DEV):
+
+        @pl.when(count > slot)
+        def _(slot=slot):
+            pltpu.make_async_copy(out_ref.at[:, slot], out_hbm.at[:, slot], sems.at[slot]).wait()
+
+
+def correlate_ahead(chosen, toeplitz, following, stacks, units):
+    owned, segments, sample_count = 4 * units, following.shape[0] // units, following.shape[2]
 
     def body(*refs):
-        correlate_kernel(units, merged_here, *refs)
-
-    scratch = [
-        pltpu.VMEM(shape, jnp.float32),
-        pltpu.SemaphoreType.DMA((PAIR_DEV,)),
-    ]
-    if merged_here:
-        own = receivers[0]
-        scratch.append(pltpu.VMEM(own.shape, own.dtype))
-        scratch.append(spread_like(own.shape[1], own.shape[3], units))
+        ahead_kernel(units, *refs)
+
     return pl.pallas_call(
         body,
-        out_shape=jax.ShapeDtypeStruct(shape, jnp.float32),
-        in_specs=[pl.BlockSpec(memory_space=pltpu.SMEM)]
-        + [pl.BlockSpec(memory_space=pltpu.VMEM)] * (1 + len(receivers)),
+        out_shape=jax.ShapeDtypeStruct(stacks.shape, stacks.dtype),
+        in_specs=[
+            pl.BlockSpec(memory_space=pltpu.SMEM),
+            pl.BlockSpec(memory_space=pltpu.VMEM),
+            pl.BlockSpec(memory_space=pltpu.VMEM),
+            pl.BlockSpec(memory_space=pl.ANY),
+        ],
         out_specs=pl.BlockSpec(memory_space=pl.ANY),
-        scratch_shapes=scratch,
+        scratch_shapes=[
+            pltpu.SMEM((PAIR_DEV,), jnp.int32),
+            pltpu.VMEM((NEAR // 2, segments, owned, sample_count), jnp.bfloat16),
+            spread_like(segments, sample_count, units),
+            pltpu.VMEM(stacks.shape, stacks.dtype),
+            pltpu.SemaphoreType.DMA((PAIR_DEV,)),
+        ],
+        input_output_aliases={3: 0},
         compiler_params=pltpu.CompilerParams(vmem_limit_bytes=KERNEL_VMEM),
-        name="correlate",
-    )(in_scalar(chosen), near_core(toeplitz), *map(near_core, receivers))
+        name="correlate_ahead",
+    )(in_scalar(chosen), near_core(toeplitz), near_core(following), stacks)
 
 
 def local(recordings, gap_start, dropout_extent, filter_taps, source_channel, receiver_block):
@@ -362,14 +415,15 @@
     sources = lax.all_gather(picked, "tm")
     if kept == 4 and owned == 4 * units and near == 2:
         toeplitz, own = prepare(channels, sources, (got,), owned, units)
-        return correlate(chosen, toeplitz, (own, following), owned, units)
+        stacks = correlate(chosen, toeplitz, own)
+        return correlate_ahead(chosen, toeplitz, following, stacks, units)
     across = owned // kept
     first = lax.axis_index("tm") * owned % units
     apart = [x.reshape(segments, units, near, kept, sample_count) for x in (got, following)]
     apart = lax.dynamic_slice_in_dim(jnp.concatenate(apart, axis=2), first, across, axis=1)
     merged = apart.transpose(2, 0, 3, 1, 4).reshape(2 * near, segments, owned, sample_count)
     (toeplitz,) = prepare(channels, sources, (), owned, units)
-    return correlate(chosen, toeplitz, (merged,), owned, units)
+    return correlate(chosen, toeplitz, merged)
 
 
 def solution(mesh):

time: 31.4 us -> 31 us (0.987)
  waiting for transfers between devices: 2.33 us -> 0.77 us
  Pallas kernels: 4.57 us -> 5.76 us
    ppermute x1, waiting for transfers between devices: 2.33 us -> 0.77 us  [local(): lax.ppermute(got, 'chan', [(group, group - 1) for group in range(1, group...]
    pallas_call x1 -> x2, Pallas kernels: 1.67 us -> 2.86 us  [the longest x1 1.55 us: correlate(): pl.pallas_call(correlate_kernel, out_shape=jax.ShapeDtypeStruct(shape, jn...]
  transfers between devices with their start and end apart: 1 -> 1, of which waited for: 1 -> 1; matrix products, arithmetic and copies ran while one was open for 0% -> 0% of each run, Pallas kernels for 3% -> 8%
where the time goes in v8:
time: 31 us; the launch traced here: 30.8 us
  blocking collectives  23 us (74%)
  Pallas kernels  5.76 us (19%)
  starting transfers between devices  1.28 us (4%)
  waiting for transfers between devices  0.77 us (2%)
    all_to_all x1, blocking collectives, local(): lax.all_to_all(sent.reshape(segments * groups, near * kept, sample_count)...  17.8 us
    all_gather x1, blocking collectives, local(): sources = lax.all_gather(picked, 'tm')  5.23 us
    pallas_call x1, Pallas kernels, normalize(): pl.pallas_call(body, out_shape=(pltpu.VMEM((slots, blocks * kept, sample_...  1.91 us
    pallas_call x1, Pallas kernels, correlate(): pl.pallas_call(correlate_kernel, out_shape=jax.ShapeDtypeStruct(shape, jn...  1.55 us
    pallas_call x1, Pallas kernels, correlate_ahead(): pl.pallas_call(body, out_shape=jax.ShapeDtypeStruct(stacks.shape, stacks....  1.31 us
    ppermute x1, starting transfers between devices, local(): lax.ppermute(got, 'chan', [(group, group - 1) for group in range(1, group...  1.28 us
    ppermute x1, waiting for transfers between devices, local(): lax.ppermute(got, 'chan', [(group, group - 1) for group in range(1, group...  0.77 us
    pallas_call x1, Pallas kernels, prepare(): pl.pallas_call(body, out_shape=out_shape, in_specs=[pl.BlockSpec(memory_s...  0.76 us
  transfers between devices with their start and end apart: 1, of which 1 were waited for; matrix products, arithmetic and copies ran while one was open for 0% of the time, Pallas kernels for 8%

profile of v8, /device:TPU:0, one launch (start us, length us, event | category | flops | bytes accessed | tf_op | source)
XLA Modules:
  0.0 30.8 jit_solution(7829567855403181922)
XLA Ops:
  0.0 1.9 %normalize.1 = (bf16[4,64,512]{2,1,0:T(8,128)(2,1)S(1)}, s32[4]{0:T(128)S(4)}, s32[4]{0:T(128)S(4)}) custom-call(f32[16,4,16,128]{3,2,1,0:T(8,128)} %bitcast.8, f32[1,128]{1,0:T(1,128)} %bitcast.11, s32[1,256]{1,0:T(1,128)} %bitcast.9, s32[1,256]{1,0:T(1,128)} %bitcast.10, s32[4]{0:T(128)} %refs_4_.1, s32[4]{0:T(128)} %refs_5_.1), custom_call_target="tpu_custom_call" | custom-call | tf_op jit(solution)/shard_map/normalize/pallas_call | solution.py:115
  1.9 17.8 %all_to_all.5.refs_1_.refs_2_ = bf16[32,8,512]{2,1,0:T(8,128)(2,1)S(1)} all-to-all(bf16[32,8,512]{2,1,0:T(8,128)(2,1)S(1)} %bitcast.7), channel_id=1, replica_groups=mesh['tm'=4,'chan'=8] {'tm','chan'}, dimensions={0} | all-to-all | bytes 524288 | tf_op jit(solution)/shard_map/all_to_all | solution.py:406
  19.7 1.3 %collective-permute-start = (bf16[32,8,512]{2,1,0:T(8,128)(2,1)S(1)}, bf16[32,8,512]{2,1,0:T(8,128)(2,1)S(1)}, u32[]{:S(2)}, u32[]{:S(2)}) collective-permute-start(bf16[32,8,512]{2,1,0:T(8,128)(2,1)S(1)} %all_to_all.5.refs_1_.refs_2_), channel_id=1, source_target_pairs={{1,0},{2,1},{3,2},{4,3},{5,4},{6,5},{7,6},{9,8},{10,9},{11,10},{12... | collective-permute-start | bytes 786440 | tf_op jit(solution)/shard_map/ppermute | solution.py:413
  21.0 0.2 pick_sources.1
  21.2 5.2 %all-gather = bf16[64,512]{1,0:T(8,128)(2,1)S(1)} all-gather(bf16[16,512]{1,0:T(8,128)(2,1)S(1)} %pick_sources.1), channel_id=2, replica_groups=mesh['tm'=4,'chan'=8] {'tm'}, dimensions={0}, use_global_device_ids=true | all-gather | bytes 81920 | tf_op jit(solution)/shard_map/all_gather | solution.py:415
  26.4 0.8 %prepare.1 = (bf16[16,128,640]{2,1,0:T(8,128)(2,1)S(1)}, bf16[2,4,32,512]{3,2,1,0:T(8,128)(2,1)S(1)}) custom-call(s32[4]{0:T(128)S(4)} %get-tuple-element.11.refs_0_, bf16[4,16,512]{2,1,0:T(8,128)(2,1)S(1)} %bitcast.6, bf16[32,8,512]{2,1,0:T(8,128)(2,1)S(1)} %all_to_all.5.refs_1_.refs_2_), custom_call_target="tpu_custom_call" | custom-call | tf_op jit(solution)/shard_map/prepare/pallas_call | solution.py:227
  27.2 1.6 %correlate.1.refs_3_ = f32[32,4,1024]{2,1,0:T(4,128)} custom-call(s32[4]{0:T(128)S(4)} %get-tuple-element.10.block_ref.refs_0_, bf16[16,128,640]{2,1,0:T(8,128)(2,1)S(1)} %get-tuple-element.13.moved_ref.refs_1_, bf16[2,4,32,512]{3,2,1,0:T(8,128)(2,1)S(1)} %get-tuple-element.14.merged_ref), custom_call_target="tpu_custom_call" | custom-call | tf_op jit(solution)/shard_map/correlate/pallas_call | solution.py:302
  28.7 0.8 %collective-permute-done.refs_2_ = bf16[32,8,512]{2,1,0:T(8,128)(2,1)S(1)} collective-permute-done((bf16[32,8,512]{2,1,0:T(8,128)(2,1)S(1)}, bf16[32,8,512]{2,1,0:T(8,128)(2,1)S(1)}, u32[]{:S(2)}, u32[]{:S(2)}) %collective-permute-start) | collective-permute-done | bytes 262176 | tf_op jit(solution)/shard_map/ppermute | solution.py:413
  29.5 1.3 %correlate_ahead.1 = f32[32,4,1024]{2,1,0:T(4,128)} custom-call(s32[4]{0:T(128)S(4)} %get-tuple-element.10.block_ref.refs_0_, bf16[16,128,640]{2,1,0:T(8,128)(2,1)S(1)} %get-tuple-element.13.moved_ref.refs_1_, bf16[32,8,512]{2,1,0:T(8,128)(2,1)S(1)} %collective-permute-done.refs_2_, f32[32,4,1024]{2,1,0:T(4,128)} %correlate.1.refs_3_), custom_call_target="tpu_custom_call", output_to_operand_aliasing={{}: (3, {})} | custom-call | tf_op jit(solution)/shard_map/correlate_ahead/pallas_call | solution.py:367
Async XLA Ops:
  19.7 9.8 %collective-permute-start = (bf16[32,8,512]{2,1,0:T(8,128)(2,1)S(1)}, bf16[32,8,512]{2,1,0:T(8,128)(2,1)S(1)}, u32[]{:S(2)}, u32[]{:S(2)}) collective-permute-start(bf16[32,8,512]{2,1,0:T(8,128)(2,1)S(1)} %all_to_all.5.refs_1_.refs_2_), channel_id=1, source_target_pairs={{1,0},{2,1},{3,2},{4,3},{5,4},{6,5},{7,6},{9,8},{10,9},{11,10},{12... | collective-permute-start | bytes 786440 | tf_op jit(solution)/shard_map/ppermute | solution.py:413

commit v9 on v7

--- a/solution.py
+++ b/solution.py
@@ -286,7 +286,7 @@
     factor = 1.0 / math.sqrt(sample_count * segments)
     if merged_here:
         merge_in_kernel(next_ref, after_ref, spread_ref, units)
-    copies = []
+    every = []
     for pair in range(PAIR_DEV):
         block = block_ref[pair]
         if merged_here:
@@ -297,10 +297,19 @@
             ]
         else:
             receivers = [merged_ref[block, i] for i in range(segments)]
-        sums = lag_products(receivers, [moved_ref[pair * segments + i] for i in range(segments)])
-        for chunk, part in enumerate(sums):
-            out_ref[:, pair, chunk * LANES : (chunk + 1) * LANES] = part * factor
-        copy = pltpu.make_async_copy(out_ref.at[:, pair], out_hbm.at[:, pair], sems.at[pair])
+        moved = [moved_ref[pair * segments + i] for i in range(segments)]
+        every.append(lag_products(receivers, moved))
+    chunks, places, _ = out_ref.shape
+    owned = places // PAIR_DEV
+    copies = []
+    for chunk in range(chunks):
+        for pair in range(PAIR_DEV):
+            out_ref[chunk, pl.ds(pair, owned, stride=PAIR_DEV), :] = every[pair][chunk] * factor
+        copy = pltpu.make_async_copy(
+            out_ref.at[chunk].reshape(owned, PAIR_DEV, LANES),
+            out_hbm.at[:, :, chunk * LANES : (chunk + 1) * LANES],
+            sems.at[chunk],
+        )
         copy.start()
         copies.append(copy)
     for copy in copies:
@@ -310,13 +319,14 @@
 def correlate(chosen, toeplitz, receivers, owned, units):
     merged_here = len(receivers) == 2
     shape = (owned, PAIR_DEV, 2 * MAX_LAG)
+    chunks = 2 * MAX_LAG // LANES
 
     def body(*refs):
         correlate_kernel(units, merged_here, *refs)
 
     scratch = [
-        pltpu.VMEM(shape, jnp.float32),
-        pltpu.SemaphoreType.DMA((PAIR_DEV,)),
+        pltpu.VMEM((chunks, owned * PAIR_DEV, LANES), jnp.float32),
+        pltpu.SemaphoreType.DMA((chunks,)),
     ]
     if merged_here:
         own = receivers[0]

time: 31.4 us -> 31.3 us (level)
  no operation moved by 1% of the time
where the time goes in v9:
time: 31.3 us; the launch traced here: 31.1 us
  blocking collectives  23 us (73%)
  Pallas kernels  4.48 us (14%)
  waiting for transfers between devices  2.33 us (7%)
  starting transfers between devices  1.28 us (4%)
    all_to_all x1, blocking collectives, local(): lax.all_to_all(sent.reshape(segments * groups, near * kept, sample_count)...  17.8 us
    all_gather x1, blocking collectives, local(): sources = lax.all_gather(picked, 'tm')  5.23 us
    ppermute x1, waiting for transfers between devices, local(): lax.ppermute(got, 'chan', [(group, group - 1) for group in range(1, group...  2.33 us
    pallas_call x1, Pallas kernels, normalize(): pl.pallas_call(body, out_shape=(pltpu.VMEM((slots, blocks * kept, sample_...  1.91 us
    pallas_call x1, Pallas kernels, correlate(): pl.pallas_call(body, out_shape=jax.ShapeDtypeStruct(shape, jnp.float32),...  1.59 us
    ppermute x1, starting transfers between devices, local(): lax.ppermute(got, 'chan', [(group, group - 1) for group in range(1, group...  1.28 us
    pallas_call x1, Pallas kernels, prepare(): pl.pallas_call(body, out_shape=out_shape, in_specs=[pl.BlockSpec(memory_s...  0.76 us
  transfers between devices with their start and end apart: 1, of which 1 were waited for; matrix products, arithmetic and copies ran while one was open for 0% of the time, Pallas kernels for 3%

profile of v9, /device:TPU:0, one launch (start us, length us, event | category | flops | bytes accessed | tf_op | source)
XLA Modules:
  0.0 31.1 jit_solution(5436742726523243087)
XLA Ops:
  0.0 1.9 %normalize.1 = (bf16[4,64,512]{2,1,0:T(8,128)(2,1)S(1)}, s32[4]{0:T(128)S(4)}, s32[4]{0:T(128)S(4)}) custom-call(f32[16,4,16,128]{3,2,1,0:T(8,128)} %bitcast.8, f32[1,128]{1,0:T(1,128)} %bitcast.11, s32[1,256]{1,0:T(1,128)} %bitcast.9, s32[1,256]{1,0:T(1,128)} %bitcast.10, s32[4]{0:T(128)} %refs_4_.1, s32[4]{0:T(128)} %refs_5_.1), custom_call_target="tpu_custom_call" | custom-call | tf_op jit(solution)/shard_map/normalize/pallas_call | solution.py:115
  1.9 17.8 %all_to_all.5.refs_1_.refs_2_ = bf16[32,8,512]{2,1,0:T(8,128)(2,1)S(1)} all-to-all(bf16[32,8,512]{2,1,0:T(8,128)(2,1)S(1)} %bitcast.7), channel_id=1, replica_groups=mesh['tm'=4,'chan'=8] {'tm','chan'}, dimensions={0} | all-to-all | bytes 524288 | tf_op jit(solution)/shard_map/all_to_all | solution.py:363
  19.7 1.3 %collective-permute-start = (bf16[32,8,512]{2,1,0:T(8,128)(2,1)S(1)}, bf16[32,8,512]{2,1,0:T(8,128)(2,1)S(1)}, u32[]{:S(2)}, u32[]{:S(2)}) collective-permute-start(bf16[32,8,512]{2,1,0:T(8,128)(2,1)S(1)} %all_to_all.5.refs_1_.refs_2_), channel_id=1, source_target_pairs={{1,0},{2,1},{3,2},{4,3},{5,4},{6,5},{7,6},{9,8},{10,9},{11,10},{12... | collective-permute-start | bytes 786440 | tf_op jit(solution)/shard_map/ppermute | solution.py:370
  21.0 0.2 pick_sources.1
  21.2 5.2 %all-gather = bf16[64,512]{1,0:T(8,128)(2,1)S(1)} all-gather(bf16[16,512]{1,0:T(8,128)(2,1)S(1)} %pick_sources.1), channel_id=2, replica_groups=mesh['tm'=4,'chan'=8] {'tm'}, dimensions={0}, use_global_device_ids=true | all-gather | bytes 81920 | tf_op jit(solution)/shard_map/all_gather | solution.py:372
  26.4 0.8 %prepare.1 = (bf16[16,128,640]{2,1,0:T(8,128)(2,1)S(1)}, bf16[2,4,32,512]{3,2,1,0:T(8,128)(2,1)S(1)}) custom-call(s32[4]{0:T(128)S(4)} %get-tuple-element.11.refs_0_, bf16[4,16,512]{2,1,0:T(8,128)(2,1)S(1)} %bitcast.6, bf16[32,8,512]{2,1,0:T(8,128)(2,1)S(1)} %all_to_all.5.refs_1_.refs_2_), custom_call_target="tpu_custom_call" | custom-call | tf_op jit(solution)/shard_map/prepare/pallas_call | solution.py:227
  27.2 2.3 %collective-permute-done.refs_3_ = bf16[32,8,512]{2,1,0:T(8,128)(2,1)S(1)} collective-permute-done((bf16[32,8,512]{2,1,0:T(8,128)(2,1)S(1)}, bf16[32,8,512]{2,1,0:T(8,128)(2,1)S(1)}, u32[]{:S(2)}, u32[]{:S(2)}) %collective-permute-start) | collective-permute-done | bytes 262176 | tf_op jit(solution)/shard_map/ppermute | solution.py:370
  29.5 1.6 %correlate.1 = f32[32,4,1024]{2,1,0:T(4,128)} custom-call(s32[4]{0:T(128)S(4)} %get-tuple-element.10.refs_0_, bf16[16,128,640]{2,1,0:T(8,128)(2,1)S(1)} %get-tuple-element.13.refs_1_, bf16[2,4,32,512]{3,2,1,0:T(8,128)(2,1)S(1)} %get-tuple-element.14.refs_2_, bf16[32,8,512]{2,1,0:T(8,128)(2,1)S(1)} %collective-permute-done.refs_3_), custom_call_target="tpu_custom_call" | custom-call | tf_op jit(solution)/shard_map/correlate/pallas_call | solution.py:335
Async XLA Ops:
  19.7 9.8 %collective-permute-start = (bf16[32,8,512]{2,1,0:T(8,128)(2,1)S(1)}, bf16[32,8,512]{2,1,0:T(8,128)(2,1)S(1)}, u32[]{:S(2)}, u32[]{:S(2)}) collective-permute-start(bf16[32,8,512]{2,1,0:T(8,128)(2,1)S(1)} %all_to_all.5.refs_1_.refs_2_), channel_id=1, source_target_pairs={{1,0},{2,1},{3,2},{4,3},{5,4},{6,5},{7,6},{9,8},{10,9},{11,10},{12... | collective-permute-start | bytes 786440 | tf_op jit(solution)/shard_map/ppermute | solution.py:370

commit v10 on v9

--- a/solution.py
+++ b/solution.py
@@ -255,14 +255,14 @@
         pairs.append(jnp.concatenate(tiles[0:pieces:2], axis=1))
         pairs.append(jnp.concatenate(tiles[1:pieces:2], axis=1))
         last.append(tiles[pieces])
+    second = jnp.dot(
+        jnp.concatenate(stacked, axis=1),
+        jnp.concatenate(last, axis=0),
+        preferred_element_type=jnp.float32,
+    )
     first = jnp.dot(
         jnp.concatenate(sides, axis=1),
         jnp.concatenate(pairs, axis=0),
-        preferred_element_type=jnp.float32,
-    )
-    second = jnp.dot(
-        jnp.concatenate(stacked, axis=1),
-        jnp.concatenate(last, axis=0),
         preferred_element_type=jnp.float32,
     )
     sums = [None] * (2 * pieces)

time: 31.3 us -> 31.3 us (level)
  no operation moved by 1% of the time
where the time goes in v10:
time: 31.3 us; the launch traced here: 31.1 us
  blocking collectives  23 us (73%)
  Pallas kernels  4.51 us (14%)
  waiting for transfers between devices  2.33 us (7%)
  starting transfers between devices  1.28 us (4%)
    all_to_all x1, blocking collectives, local(): lax.all_to_all(sent.reshape(segments * groups, near * kept, sample_count)...  17.8 us
    all_gather x1, blocking collectives, local(): sources = lax.all_gather(picked, 'tm')  5.23 us
    ppermute x1, waiting for transfers between devices, local(): lax.ppermute(got, 'chan', [(group, group - 1) for group in range(1, group...  2.33 us
    pallas_call x1, Pallas kernels, normalize(): pl.pallas_call(body, out_shape=(pltpu.VMEM((slots, blocks * kept, sample_...  1.91 us
    pallas_call x1, Pallas kernels, correlate(): pl.pallas_call(body, out_shape=jax.ShapeDtypeStruct(shape, jnp.float32),...  1.61 us
    ppermute x1, starting transfers between devices, local(): lax.ppermute(got, 'chan', [(group, group - 1) for group in range(1, group...  1.28 us
    pallas_call x1, Pallas kernels, prepare(): pl.pallas_call(body, out_shape=out_shape, in_specs=[pl.BlockSpec(memory_s...  0.76 us
  transfers between devices with their start and end apart: 1, of which 1 were waited for; matrix products, arithmetic and copies ran while one was open for 0% of the time, Pallas kernels for 3%

profile of v10, /device:TPU:0, one launch (start us, length us, event | category | flops | bytes accessed | tf_op | source)
XLA Modules:
  0.0 31.1 jit_solution(6576538977750020002)
XLA Ops:
  0.0 1.9 %normalize.1 = (bf16[4,64,512]{2,1,0:T(8,128)(2,1)S(1)}, s32[4]{0:T(128)S(4)}, s32[4]{0:T(128)S(4)}) custom-call(f32[16,4,16,128]{3,2,1,0:T(8,128)} %bitcast.8, f32[1,128]{1,0:T(1,128)} %bitcast.11, s32[1,256]{1,0:T(1,128)} %bitcast.9, s32[1,256]{1,0:T(1,128)} %bitcast.10, s32[4]{0:T(128)} %refs_4_.1, s32[4]{0:T(128)} %refs_5_.1), custom_call_target="tpu_custom_call" | custom-call | tf_op jit(solution)/shard_map/normalize/pallas_call | solution.py:115
  1.9 17.8 %all_to_all.5.refs_1_.refs_2_ = bf16[32,8,512]{2,1,0:T(8,128)(2,1)S(1)} all-to-all(bf16[32,8,512]{2,1,0:T(8,128)(2,1)S(1)} %bitcast.7), channel_id=1, replica_groups=mesh['tm'=4,'chan'=8] {'tm','chan'}, dimensions={0} | all-to-all | bytes 524288 | tf_op jit(solution)/shard_map/all_to_all | solution.py:363
  19.7 1.3 %collective-permute-start = (bf16[32,8,512]{2,1,0:T(8,128)(2,1)S(1)}, bf16[32,8,512]{2,1,0:T(8,128)(2,1)S(1)}, u32[]{:S(2)}, u32[]{:S(2)}) collective-permute-start(bf16[32,8,512]{2,1,0:T(8,128)(2,1)S(1)} %all_to_all.5.refs_1_.refs_2_), channel_id=1, source_target_pairs={{1,0},{2,1},{3,2},{4,3},{5,4},{6,5},{7,6},{9,8},{10,9},{11,10},{12... | collective-permute-start | bytes 786440 | tf_op jit(solution)/shard_map/ppermute | solution.py:370
  21.0 0.2 pick_sources.1
  21.2 5.2 %all-gather = bf16[64,512]{1,0:T(8,128)(2,1)S(1)} all-gather(bf16[16,512]{1,0:T(8,128)(2,1)S(1)} %pick_sources.1), channel_id=2, replica_groups=mesh['tm'=4,'chan'=8] {'tm'}, dimensions={0}, use_global_device_ids=true | all-gather | bytes 81920 | tf_op jit(solution)/shard_map/all_gather | solution.py:372
  26.4 0.8 %prepare.1 = (bf16[16,128,640]{2,1,0:T(8,128)(2,1)S(1)}, bf16[2,4,32,512]{3,2,1,0:T(8,128)(2,1)S(1)}) custom-call(s32[4]{0:T(128)S(4)} %get-tuple-element.11.refs_0_, bf16[4,16,512]{2,1,0:T(8,128)(2,1)S(1)} %bitcast.6, bf16[32,8,512]{2,1,0:T(8,128)(2,1)S(1)} %all_to_all.5.refs_1_.refs_2_), custom_call_target="tpu_custom_call" | custom-call | tf_op jit(solution)/shard_map/prepare/pallas_call | solution.py:227
  27.2 2.3 %collective-permute-done.refs_3_ = bf16[32,8,512]{2,1,0:T(8,128)(2,1)S(1)} collective-permute-done((bf16[32,8,512]{2,1,0:T(8,128)(2,1)S(1)}, bf16[32,8,512]{2,1,0:T(8,128)(2,1)S(1)}, u32[]{:S(2)}, u32[]{:S(2)}) %collective-permute-start) | collective-permute-done | bytes 262176 | tf_op jit(solution)/shard_map/ppermute | solution.py:370
  29.5 1.6 %correlate.1 = f32[32,4,1024]{2,1,0:T(4,128)} custom-call(s32[4]{0:T(128)S(4)} %get-tuple-element.10.refs_0_, bf16[16,128,640]{2,1,0:T(8,128)(2,1)S(1)} %get-tuple-element.13.refs_1_, bf16[2,4,32,512]{3,2,1,0:T(8,128)(2,1)S(1)} %get-tuple-element.14.refs_2_, bf16[32,8,512]{2,1,0:T(8,128)(2,1)S(1)} %collective-permute-done.refs_3_), custom_call_target="tpu_custom_call" | custom-call | tf_op jit(solution)/shard_map/correlate/pallas_call | solution.py:335
Async XLA Ops:
  19.7 9.8 %collective-permute-start = (bf16[32,8,512]{2,1,0:T(8,128)(2,1)S(1)}, bf16[32,8,512]{2,1,0:T(8,128)(2,1)S(1)}, u32[]{:S(2)}, u32[]{:S(2)}) collective-permute-start(bf16[32,8,512]{2,1,0:T(8,128)(2,1)S(1)} %all_to_all.5.refs_1_.refs_2_), channel_id=1, source_target_pairs={{1,0},{2,1},{3,2},{4,3},{5,4},{6,5},{7,6},{9,8},{10,9},{11,10},{12... | collective-permute-start | bytes 786440 | tf_op jit(solution)/shard_map/ppermute | solution.py:370
